TPU v7x, 32 devices: a whole 2x2x4 slice. The times are simulated.
32 devices in a mesh: dp: 4 (over y, x), mp: 8 (over z, core).
Axes of the slice: x: 2, y: 2, z: 4, core: 2. Of those that a mesh axis runs over, the one named last changes fastest.
Arguments:
- tokens: bfloat16 [1024, 4096], P('dp', 'mp'), may hold values from -6 to 6
- cotangent: bfloat16 [1024, 4096], P('dp', 'mp'), may hold values from -6 to 6
- gate_weight: bfloat16 [4096, 16384], P('dp', 'mp'), may hold values from -0.1875 to 0.1875
- up_weight: bfloat16 [4096, 16384], P('dp', 'mp'), may hold values from -0.1875 to 0.1875
- down_weight: bfloat16 [16384, 4096], P('mp', 'dp'), may hold values from -0.09375 to 0.09375
- gate_mask: int32 [32, 128], P('dp', 'mp'), may hold values from 0 to 1, as said below
- up_mask: int32 [32, 128], P('dp', 'mp'), may hold values from 0 to 1, as said below
- down_mask: int32 [128, 32], P('mp', 'dp'), may hold values from 0 to 1, as said below
Outputs:
- layer_out: bfloat16 [1024, 4096], P('dp', 'mp')
- token_grad: bfloat16 [1024, 4096], P('dp', 'mp')
- gate_grad: bfloat16 [4096, 16384], P('dp', 'mp')
- up_grad: bfloat16 [4096, 16384], P('dp', 'mp')
- down_grad: bfloat16 [16384, 4096], P('mp', 'dp')
Inputs may be any that keep to these rules, and one draw needn't show every extreme that they name: `gate_mask`: each device's part of the mask (8 x 16 blocks) has 1 to 64 nonzero blocks; in every draw all parts of one index of mp, chosen by the seed, have exactly 64, the same index for the three masks. `up_mask`: each device's part of the mask (8 x 16 blocks) has 1 to 64 nonzero blocks; in every draw all parts of one index of mp, chosen by the seed, have exactly 64, the same index for the three masks. `down_mask`: each device's part of the mask (16 x 8 blocks) has 1 to 64 nonzero blocks; in every draw all parts of one index of mp, chosen by the seed, have exactly 64, the same index for the three masks.
All inputs are finite; a program needn't handle non-finite values.
Results may differ from a plain program's by a relative error of at most 0.017.
Values may be sent and summed in bfloat16 or wider, within the bound.
No kernel may reach another device: no remote copies, remote signals or barrier semaphores. Data moves between devices by JAX's collectives and lax.ppermute only.
A program may use at most 192 MiB of HBM per device.

v0:
```python
import math

import jax
import jax.numpy as jnp
from jax import lax
from jax.experimental import pallas as pl
from jax.experimental.pallas import tpu as pltpu
from jax.sharding import PartitionSpec as P


BLK = 128
COLORS = 2
bf16, f32 = jnp.bfloat16, jnp.float32
NN = (((1,), (0,)), ((), ()))
NT = (((1,), (1,)), ((), ()))
TN = (((0,), (0,)), ((), ()))


DEPTH = 2
CHUNKS = 2


def after(value, *earlier):
    return lax.optimization_barrier((value,) + earlier)[0]


def dot(a, b, dims):
    return lax.dot_general(a, b, dims, preferred_element_type=f32)


def keep_blocks(dst, value_of, mask, row0, col0):
    for rb in range(dst.shape[0] // BLK):
        for cb in range(dst.shape[1] // BLK):
            at = (slice(rb * BLK, (rb + 1) * BLK), slice(cb * BLK, (cb + 1) * BLK))
            block = value_of(at)
            dst[at] = jnp.where(mask[row0 + rb, col0 + cb] != 0, block, jnp.zeros_like(block))


def load_groups(places, sems):
    copies = [pltpu.make_async_copy(src, dst, sems.at[n]) for n, (src, dst) in enumerate(places)]
    for copy in copies:
        copy.start()
    for copy in copies:
        copy.wait()


def by_group(refs, held, rows, half):
    groups = len(refs) // COLORS
    places = []
    for n, ref in enumerate(refs):
        color, k = divmod(n, groups)
        places.append((ref, held.at[pl.ds(k * rows, rows), pl.ds(color * half, half)]))
    return places


def by_chunk(refs, pick, held, rows, half, chunks):
    per = len(refs) // chunks
    groups = per // COLORS
    places = []
    for n, ref in enumerate(refs):
        j, rest = divmod(n, per)
        color, k = divmod(rest, groups)
        at = pl.ds((k * chunks + j) * rows, rows)
        places.append((ref.at[pick], held.at[at, pl.ds(color * half, half)]))
    return places


def call(kernel, grid, prefetch, in_specs, out_specs, out_shape, scratch, flops, nbytes, args, limit=40000):
    return pl.pallas_call(
        kernel,
        grid_spec=pltpu.PrefetchScalarGridSpec(
            num_scalar_prefetch=len(prefetch),
            grid=grid,
            in_specs=in_specs,
            out_specs=out_specs,
            scratch_shapes=scratch,
        ),
        out_shape=out_shape,
        compiler_params=pltpu.CompilerParams(
            dimension_semantics=("arbitrary",) * len(grid), vmem_limit_bytes=limit << 10
        ),
        cost_estimate=pl.CostEstimate(flops=flops, transcendentals=0, bytes_accessed=nbytes),
    )(*prefetch, *args)


def whole_spec(shape):
    return pl.BlockSpec(shape, lambda *_: (0,) * len(shape))


ANY = pl.BlockSpec(memory_space=pl.ANY)


def project(x, weight, mask, color, turned):
    groups, r, rows, cols = x.shape
    depth, fan = weight.shape[::-1] if turned else weight.shape
    half = fan // COLORS
    tile = min(half, 512)
    base = color * half // tile

    def kernel(mask_ref, x_ref, w_ref, *rest):
        outs, kept = rest[:groups], rest[groups]
        first = (base + pl.program_id(0)) * (tile // BLK)
        if turned:
            keep_blocks(kept, lambda at: w_ref[at], mask_ref, first, 0)
        else:
            keep_blocks(kept, lambda at: w_ref[at], mask_ref, 0, first)
        total = None
        for c in range(r):
            left = x_ref[:, c].reshape(groups * rows, cols)
            span = slice(c * cols, (c + 1) * cols)
            term = dot(left, kept[:, span], NT) if turned else dot(left, kept[span, :], NN)
            total = term if total is None else total + term
        for k in range(groups):
            outs[k][...] = total[k * rows : (k + 1) * rows].astype(bf16)

    shape = (tile, depth) if turned else (depth, tile)
    index = (lambda n, m: (base + n, 0)) if turned else (lambda n, m: (0, base + n))
    return call(
        kernel,
        (half // tile,),
        [mask],
        [whole_spec(x.shape), pl.BlockSpec(shape, index)],
        [pl.BlockSpec((rows, tile), lambda n, m: (0, n))] * groups,
        [jax.ShapeDtypeStruct((rows, half), bf16)] * groups,
        [pltpu.VMEM(shape, bf16)],
        2 * groups * rows * depth * half,
        2 * (groups * rows * depth + depth * half + groups * rows * half),
        [x, weight],
        limit=24000,
    )


def back_project(parts, weights, masks, place, r, turned):
    groups = len(parts) // COLORS
    rows, half = parts[0].shape[-2:]
    fan = half * COLORS
    depth = weights[0].shape[0] if turned else weights[0].shape[1]
    cols = depth // r
    tile = min(cols, 256)
    sub = cols // tile
    count, several = len(parts), len(weights)

    def tile_at(s, u, place_ref):
        return (s ^ place_ref[0]) * sub + u

    def kernel(place_ref, *rest):
        mask_refs, rest = rest[:several], rest[several:]
        part_refs, rest = rest[:count], rest[count:]
        w_refs, rest = rest[:several], rest[several:]
        outs, rest = rest[:r], rest[r:]
        helds, kepts, sems = rest[:several], rest[several : 2 * several], rest[2 * several]
        s, u = pl.program_id(0), pl.program_id(1)

        @pl.when((s == 0) & (u == 0))
        def _():
            places = []
            for i in range(several):
                if several > 1:
                    places += by_chunk(part_refs, i, helds[i], rows, half, 1)
                else:
                    places += by_group(part_refs, helds[i], rows, half)
            load_groups(places, sems)

        first = tile_at(s, u, place_ref) * (tile // BLK)
        total = None
        for i in range(several):
            w_ref = w_refs[i]
            where = (first, 0) if turned else (0, first)
            keep_blocks(kepts[i], lambda at: w_ref[at], mask_refs[i], *where)
            term = dot(helds[i][...], kepts[i][...], NT if turned else NN)
            total = term if total is None else total + term
        total = total.astype(bf16).reshape(groups, rows, tile)
        for t in range(r):

            @pl.when(s == t)
            def _():
                outs[t][...] = total

    def share(t):
        return lambda s, u, *_: (0, 0, jnp.where(s == t, u, jnp.where(s < t, 0, sub - 1)))

    shape = (tile, fan) if turned else (fan, tile)
    if turned:
        index = lambda s, u, pr, *_: (tile_at(s, u, pr), 0)
    else:
        index = lambda s, u, pr, *_: (0, tile_at(s, u, pr))
    return call(
        kernel,
        (r, sub),
        [place] + masks,
        [ANY] * count + [pl.BlockSpec(shape, index)] * several,
        [pl.BlockSpec((groups, rows, tile), share(t)) for t in range(r)],
        [jax.ShapeDtypeStruct((groups, rows, cols), bf16)] * r,
        [pltpu.VMEM((groups * rows, fan), bf16)] * several
        + [pltpu.VMEM(shape, bf16)] * several
        + [pltpu.SemaphoreType.DMA((count * several,))],
        2 * several * groups * rows * depth * fan,
        2 * several * (groups * rows * fan + depth * fan) + 2 * groups * rows * depth,
        list(parts) + list(weights),
    )


def outer_up(x, parts, pick, chunks, mask, scale):
    groups, r, rows, cols = x.shape
    half = parts[0].shape[-1]
    fan, depth = half * COLORS, r * cols
    tile = min(cols, 256)
    sub = cols // tile

    def kernel(mask_ref, x_ref, *rest):
        part_refs, (out, held, sems) = rest[: len(parts)], rest[len(parts) :]
        n = pl.program_id(0)

        @pl.when(n == 0)
        def _():
            load_groups(by_chunk(part_refs, pick, held, rows // chunks, half, chunks), sems)

        left = x_ref[:, 0].reshape(groups * rows, tile)
        value = dot(left, held[...], TN) * scale
        keep_blocks(out, lambda at: value[at].astype(bf16), mask_ref, n * (tile // BLK), 0)

    return call(
        kernel,
        (depth // tile,),
        [mask],
        [pl.BlockSpec((groups, 1, rows, tile), lambda n, m: (0, n // sub, 0, n % sub))]
        + [ANY] * len(parts),
        pl.BlockSpec((tile, fan), lambda n, m: (n, 0)),
        jax.ShapeDtypeStruct((depth, fan), bf16),
        [pltpu.VMEM((groups * rows, fan), bf16), pltpu.SemaphoreType.DMA((len(parts),))],
        2 * groups * rows * depth * fan,
        2 * (groups * rows * (depth + fan) + depth * fan),
        [x] + list(parts),
    )


def outer_down(parts, x, mask, scale):
    groups, r, rows, cols = x.shape
    half = parts[0].shape[1]
    fan, depth = half * COLORS, r * cols
    tile = min(fan, 256)

    def kernel(mask_ref, x_ref, *rest):
        part_refs, (out, held, sems) = rest[: len(parts)], rest[len(parts) :]
        n = pl.program_id(0)

        @pl.when(n == 0)
        def _():
            load_groups(by_group(part_refs, held, rows, half), sems)

        left = held[:, pl.ds(pl.multiple_of(n * tile, tile), tile)]
        for c in range(r):
            value = dot(left, x_ref[:, c].reshape(groups * rows, cols), TN) * scale
            keep_blocks(
                out.at[:, pl.ds(c * cols, cols)],
                lambda at: value[at].astype(bf16),
                mask_ref,
                n * (tile // BLK),
                c * (cols // BLK),
            )

    return call(
        kernel,
        (fan // tile,),
        [mask],
        [whole_spec(x.shape)] + [ANY] * len(parts),
        pl.BlockSpec((tile, depth), lambda n, m: (n, 0)),
        jax.ShapeDtypeStruct((fan, depth), bf16),
        [pltpu.VMEM((groups * rows, fan), bf16), pltpu.SemaphoreType.DMA((len(parts),))],
        2 * groups * rows * depth * fan,
        2 * (groups * rows * (depth + fan) + depth * fan),
        [x] + list(parts),
    )


def assemble(pieces, where, groups, r):
    rows, cols = pieces[0][0].shape
    flat = [p for line in pieces for p in line]

    def kernel(where_ref, *rest):
        refs, (out, sems) = rest[: len(flat)], rest[len(flat) :]
        copies = []
        for n, ref in enumerate(refs):
            s, t = divmod(n, groups)
            dst = out.at[where_ref[0] ^ t, where_ref[1] ^ s]
            copies.append(pltpu.make_async_copy(ref, dst, sems.at[n]))
        for copy in copies:
            copy.start()
        for copy in copies:
            copy.wait()

    return call(
        kernel,
        (1,),
        [where],
        [ANY] * len(flat),
        whole_spec((groups, r, rows, cols)),
        jax.ShapeDtypeStruct((groups, r, rows, cols), bf16),
        [pltpu.SemaphoreType.DMA((len(flat),))],
        0,
        4 * len(flat) * rows * cols,
        flat,
    )


def body(tokens, cotangent, gate_weight, up_weight, down_weight, gate_mask, up_mask, down_mask):
    dp = lax.axis_size("dp")
    mp = lax.axis_size("mp")
    ratio = mp // dp
    bits = dp.bit_length() - 1
    rows = tokens.shape[0]
    scale = 1.0 / math.sqrt(rows * dp)
    there = []
    for i in range(dp):
        for j in range(mp):
            d, c = j // ratio, j % ratio
            there.append((i * mp + j, d * mp + ratio * (i ^ d) + c))
    back = [(b, a) for a, b in there]
    me = lax.axis_index("mp")
    my_k, my_c = me // ratio, me % ratio
    where = jnp.stack([my_k, my_c]).astype(jnp.int32)
    place = my_c.reshape(1).astype(jnp.int32)

    def over_mp(value, step):
        return lax.ppermute(value, "mp", [(j, j ^ step) for j in range(mp)])

    queues = [[] for _ in range(bits)]

    def over_dp(value, bit, *earlier):
        queue = queues[bit]
        earlier = list(earlier)
        if len(queue) >= DEPTH:
            earlier.append(queue[-DEPTH])
        if earlier:
            value = after(value, *earlier)
        queue.append(lax.ppermute(value, "dp", [(i, i ^ (1 << bit)) for i in range(dp)]))
        return queue[-1]

    def spread_rows(moved):
        line = [moved] + [over_mp(moved, ratio * t) for t in range(1, dp)]
        pieces = [line] + [[over_mp(v, s) for v in line] for s in range(1, ratio)]
        return assemble(pieces, where, dp, ratio), line

    def collect_rows(part):
        total = part[0].astype(f32)
        for s in range(1, ratio):
            total = total + over_mp(part[s], s).astype(f32)
        total = total.astype(bf16)
        own = lax.dynamic_index_in_dim(total, my_k, 0, keepdims=False).astype(f32)
        for t in range(1, dp):
            sent = lax.dynamic_index_in_dim(total, my_k ^ t, 0, keepdims=False)
            own = own + over_mp(sent, ratio * t).astype(f32)
        return lax.ppermute(own.astype(bf16), ("dp", "mp"), back)

    def order(color):
        return list(range(bits)) if color % 2 == 0 else list(range(bits))[::-1]

    def reduce_dp(parts):
        vals = [dict(enumerate(p)) for p in parts]
        for step in range(bits):
            for h, held in enumerate(vals):
                bit = order(h)[step]
                for k in sorted((k for k in held if k >> bit & 1), reverse=True):
                    got = over_dp(held.pop(k).astype(bf16), bit)
                    held[k ^ (1 << bit)] = held[k ^ (1 << bit)].astype(f32) + got.astype(f32)
        return [held[0] for held in vals]

    def gather_dp(own, first=(), second=(), relay=()):
        vals = [{0: v} for v in own]
        for step in range(bits):
            for h, held in enumerate(vals):
                bit = order(h)[::-1][step]
                for k in sorted(held):
                    hold = first if step == 0 else relay if k else second
                    slot = k ^ (1 << bit)
                    held[slot] = over_dp(held[k], bit, *hold)
        return [held[k] for held in vals for k in range(dp)]

    colors = range(COLORS)
    tok_moved = lax.ppermute(tokens, ("dp", "mp"), there)
    cot_moved = lax.ppermute(cotangent, ("dp", "mp"), there)
    tok, tok_line = spread_rows(tok_moved)
    gate_parts = [project(tok, gate_weight, gate_mask, h, False) for h in colors]
    tok_up = after(tok, *[p[0] for p in gate_parts])
    up_parts = [project(tok_up, up_weight, up_mask, h, False) for h in colors]
    cot, _ = spread_rows(after(cot_moved, *tok_line, up_parts[0][0]))
    grad_parts = [project(cot, down_weight, down_mask, h, True) for h in colors]
    gate_pre = reduce_dp(gate_parts)
    up_pre = reduce_dp(up_parts)
    hidden_grad = reduce_dp(grad_parts)
    own_hidden, own_delta = [], [[] for _ in range(CHUNKS)]
    step = rows // CHUNKS
    for gate, up, grad in zip(gate_pre, up_pre, hidden_grad):
        sigmoid_gate = 1.0 / (1.0 + jnp.exp(-gate))
        activated = gate * sigmoid_gate
        own_hidden.append((activated * up).astype(bf16))
        slope = sigmoid_gate * (1.0 + gate * (1.0 - sigmoid_gate))
        gate_delta = (grad * up * slope).astype(bf16)
        up_delta = (grad * activated).astype(bf16)
        for j in range(CHUNKS):
            at = slice(j * step, (j + 1) * step)
            own_delta[j].append(jnp.stack([gate_delta[at], up_delta[at]]))
    hidden = gather_dp(own_hidden)
    out_part = back_project(hidden, [down_weight], [down_mask], place, ratio, False)
    down_grad = outer_down(hidden, cot, down_mask, scale)
    layer_out = collect_rows(out_part)
    deltas, token_grad, done = [], [], ()
    for j in range(CHUNKS):
        if j == 0:
            delta = gather_dp(own_delta[j])
        else:
            delta = gather_dp(own_delta[j], (), (out_part[0],), (out_part[0], down_grad))
        first = after(delta[0], *done)
        part = back_project(
            [first] + delta[1:],
            [gate_weight, up_weight],
            [gate_mask, up_mask],
            place,
            ratio,
            True,
        )
        token_grad.append(collect_rows(part))
        deltas += delta
        done = (layer_out, part[0])
    last_tok = after(tok, part[0])
    gate_grad = outer_up(last_tok, deltas, 0, CHUNKS, gate_mask, scale)
    up_grad = outer_up(last_tok, deltas, 1, CHUNKS, up_mask, scale)
    token_grad = jnp.concatenate(token_grad, axis=0)
    return (layer_out, token_grad, gate_grad, up_grad, down_grad)


def solution(mesh):
    placed = (
        P("dp", "mp"),
        P("dp", "mp"),
        P("dp", "mp"),
        P("dp", "mp"),
        P("mp", "dp"),
        P("dp", "mp"),
        P("dp", "mp"),
        P("mp", "dp"),
    )

    return jax.shard_map(
        body,
        mesh=mesh,
        in_specs=placed,
        out_specs=(P("dp", "mp"), P("dp", "mp"), P("dp", "mp"), P("dp", "mp"), P("mp", "dp")),
        check_vma=False,
    )
```

profile of v0, /device:TPU:6, one launch (start us, length us, event | category | flops | bytes accessed | tf_op | source)
XLA Modules:
  0.0 374.7 jit_solution(3849000438797768461)
XLA Ops:
  0.6 5.4 %collective-permute-start = (bf16[256,512]{1,0:T(8,128)(2,1)}, bf16[256,512]{1,0:T(8,128)(2,1)S(1)}, u32[]{:S(2)}, u32[]{:S(2)}) collective-permute-start(bf16[256,512]{1,0:T(8,128)(2,1)} %param.8), channel_id=1, source_target_pairs={{0,0},{1,1},{2,10},{3,11},{4,20},{5,21},{6,30},{7,31},{8,2},{9,3},... | collective-permute-start | bytes 786440 | tf_op jit(solution)/shard_map/ppermute | solution.py:380
  6.1 6.7 %collective-permute-done.rest_0_ = bf16[256,512]{1,0:T(8,128)(2,1)S(1)} collective-permute-done((bf16[256,512]{1,0:T(8,128)(2,1)}, bf16[256,512]{1,0:T(8,128)(2,1)S(1)}, u32[]{:S(2)}, u32[]{:S(2)}) %collective-permute-start) | collective-permute-done | bytes 262176 | tf_op jit(solution)/shard_map/ppermute | solution.py:380
  15.3 12.8 %collective-permute-start.2 = (bf16[256,512]{1,0:T(8,128)(2,1)S(1)}, bf16[256,512]{1,0:T(8,128)(2,1)S(1)}, u32[]{:S(2)}, u32[]{:S(2)}) collective-permute-start(bf16[256,512]{1,0:T(8,128)(2,1)S(1)} %collective-permute-done.rest_0_), channel_id=1, source_target_pairs={{0,4},{1,5},{2,6},{3,7},{4,0},{5,1},{6,2},{7,3},{8,12},{9,13},{10,... | collective-permute-start | bytes 786440 | tf_op jit(solution)/shard_map/ppermute | solution.py:325
  28.6 11.3 %collective-permute-done.2.rest_2_ = bf16[256,512]{1,0:T(8,128)(2,1)S(1)} collective-permute-done((bf16[256,512]{1,0:T(8,128)(2,1)S(1)}, bf16[256,512]{1,0:T(8,128)(2,1)S(1)}, u32[]{:S(2)}, u32[]{:S(2)}) %collective-permute-start.2) | collective-permute-done | bytes 262176 | tf_op jit(solution)/shard_map/ppermute | solution.py:325
  54.6 7.1 %collective-permute-start.18 = (bf16[256,512]{1,0:T(8,128)(2,1)S(1)}, bf16[256,512]{1,0:T(8,128)(2,1)S(1)}, u32[]{:S(2)}, u32[]{:S(2)}) collective-permute-start(bf16[256,512]{1,0:T(8,128)(2,1)S(1)} %copy-done.57), channel_id=1, source_target_pairs={{0,0},{1,1},{2,10},{3,11},{4,20},{5,21},{6,30},{7,31},{8,2},{9,3},... | collective-permute-start | bytes 786440 | tf_op jit(solution)/shard_map/ppermute | solution.py:381
  71.0 5.2 %collective-permute-start.15 = (bf16[256,1024]{1,0:T(8,128)(2,1)S(1)}, bf16[256,1024]{1,0:T(8,128)(2,1)S(1)}, u32[]{:S(2)}, u32[]{:S(2)}) collective-permute-start(bf16[256,1024]{1,0:T(8,128)(2,1)S(1)} %get-tuple-element.88), channel_id=1, source_target_pairs={{0,16},{8,24},{16,0},{24,8},{1,17},{9,25},{17,1},{25,9},{2,18},{10... | collective-permute-start | bytes 1572872 | tf_op jit(solution)/shard_map/ppermute | solution.py:336
  79.2 5.0 %collective-permute-start.19 = (bf16[256,512]{1,0:T(8,128)(2,1)S(1)}, bf16[256,512]{1,0:T(8,128)(2,1)}, u32[]{:S(2)}, u32[]{:S(2)}) collective-permute-start(bf16[256,512]{1,0:T(8,128)(2,1)S(1)} %collective-permute-done.18.rest_0_), channel_id=1, source_target_pairs={{0,2},{1,3},{2,0},{3,1},{4,6},{5,7},{6,4},{7,5},{8,10},{9,11},{10,... | collective-permute-start | bytes 786440 | tf_op jit(solution)/shard_map/ppermute | solution.py:325
  85.9 10.0 %collective-permute-done.20.rest_2_ = bf16[256,512]{1,0:T(8,128)(2,1)S(1)} collective-permute-done((bf16[256,512]{1,0:T(8,128)(2,1)S(1)}, bf16[256,512]{1,0:T(8,128)(2,1)S(1)}, u32[]{:S(2)}, u32[]{:S(2)}) %collective-permute-start.20) | collective-permute-done | bytes 262176 | tf_op jit(solution)/shard_map/ppermute | solution.py:325
  106.9 4.8 %collective-permute-start.14 = (bf16[256,1024]{1,0:T(8,128)(2,1)}, bf16[256,1024]{1,0:T(8,128)(2,1)}, u32[]{:S(2)}, u32[]{:S(2)}) collective-permute-start(bf16[256,1024]{1,0:T(8,128)(2,1)} %get-tuple-element.86), channel_id=1, source_target_pairs={{0,8},{8,0},{16,24},{24,16},{1,9},{9,1},{17,25},{25,17},{2,10},{10... | collective-permute-start | bytes 1572872 | tf_op jit(solution)/shard_map/ppermute | solution.py:336
  129.2 6.8 %collective-permute-done.13 = bf16[256,1024]{1,0:T(8,128)(2,1)} collective-permute-done((bf16[256,1024]{1,0:T(8,128)(2,1)}, bf16[256,1024]{1,0:T(8,128)(2,1)}, u32[]{:S(2)}, u32[]{:S(2)}) %collective-permute-start.13) | collective-permute-done | bytes 524320 | tf_op jit(solution)/shard_map/ppermute | solution.py:336
  149.2 9.2 %collective-permute-done.28 = bf16[256,1024]{1,0:T(8,128)(2,1)S(1)} collective-permute-done((bf16[256,1024]{1,0:T(8,128)(2,1)S(1)}, bf16[256,1024]{1,0:T(8,128)(2,1)S(1)}, u32[]{:S(2)}, u32[]{:S(2)}) %collective-permute-start.28) | collective-permute-done | bytes 524320 | tf_op jit(solution)/shard_map/ppermute | solution.py:336
  158.8 9.3 %collective-permute-done.17 = bf16[256,1024]{1,0:T(8,128)(2,1)S(1)} collective-permute-done((bf16[256,1024]{1,0:T(8,128)(2,1)S(1)}, bf16[256,1024]{1,0:T(8,128)(2,1)S(1)}, u32[]{:S(2)}, u32[]{:S(2)}) %collective-permute-start.17) | collective-permute-done | bytes 524320 | tf_op jit(solution)/shard_map/ppermute | solution.py:336
  169.7 9.7 %collective-permute-done.37 = bf16[256,1024]{1,0:T(8,128)(2,1)S(1)} collective-permute-done((bf16[256,1024]{1,0:T(8,128)(2,1)S(1)}, bf16[256,1024]{1,0:T(8,128)(2,1)S(1)}, u32[]{:S(2)}, u32[]{:S(2)}) %collective-permute-start.37) | collective-permute-done | bytes 524320 | tf_op jit(solution)/shard_map/ppermute | solution.py:336
  181.7 6.1 %collective-permute-done.31 = bf16[256,1024]{1,0:T(8,128)(2,1)S(1)} collective-permute-done((bf16[256,1024]{1,0:T(8,128)(2,1)S(1)}, bf16[256,1024]{1,0:T(8,128)(2,1)S(1)}, u32[]{:S(2)}, u32[]{:S(2)}) %collective-permute-start.31) | collective-permute-done | bytes 524320 | tf_op jit(solution)/shard_map/ppermute | solution.py:336
  193.2 9.4 %collective-permute-done.32.rest_3_.rest_2_ = bf16[256,1024]{1,0:T(8,128)(2,1)S(1)} collective-permute-done((bf16[256,1024]{1,0:T(8,128)(2,1)S(1)}, bf16[256,1024]{1,0:T(8,128)(2,1)S(1)}, u32[]{:S(2)}, u32[]{:S(2)}) %collective-permute-start.32) | collective-permute-done | bytes 524320 | tf_op jit(solution)/shard_map/ppermute | solution.py:336
  207.1 8.2 %collective-permute-done.30.rest_2_.rest_1_ = bf16[256,1024]{1,0:T(8,128)(2,1)S(1)} collective-permute-done((bf16[256,1024]{1,0:T(8,128)(2,1)S(1)}, bf16[256,1024]{1,0:T(8,128)(2,1)S(1)}, u32[]{:S(2)}, u32[]{:S(2)}) %collective-permute-start.30) | collective-permute-done | bytes 524320 | tf_op jit(solution)/shard_map/ppermute | solution.py:336
  215.3 7.4 %collective-permute-done.36.rest_4_.rest_3_ = bf16[256,1024]{1,0:T(8,128)(2,1)S(1)} collective-permute-done((bf16[256,1024]{1,0:T(8,128)(2,1)S(1)}, bf16[256,1024]{1,0:T(8,128)(2,1)S(1)}, u32[]{:S(2)}, u32[]{:S(2)}) %collective-permute-start.36) | collective-permute-done | bytes 524320 | tf_op jit(solution)/shard_map/ppermute | solution.py:336
  222.7 8.5 %shard_map.127 = (bf16[4,256,512]{2,1,0:T(8,128)(2,1)S(1)}, bf16[4,256,512]{2,1,0:T(8,128)(2,1)}) custom-call(s32[1]{0:T(128)} %bitcast.place_ref, s32[16,8]{1,0:T(8,128)S(1)} %copy.15.mask_ref.rest_0_, bf16[256,1024]{1,0:T(8,128)(2,1)S(1)} %get-tuple-element.103.rest_1_.rest_0_, bf16[256,1024]{1,0:T(8,128)(2,1)S(1)} %collective-permute-done.30.rest_2_.rest_1_, ...), custom_call_target="tpu_custom_call" | custom-call | flops 4294967296 | bytes 10485760 | tf_op jit(solution)/shard_map/pallas_call | solution.py:69
  239.2 9.8 %collective-permute-done.47.rest_7_.rest_5_ = bf16[2,128,1024]{2,1,0:T(8,128)(2,1)} collective-permute-done((bf16[2,128,1024]{2,1,0:T(8,128)(2,1)}, bf16[2,128,1024]{2,1,0:T(8,128)(2,1)}, u32[]{:S(2)}, u32[]{:S(2)}) %collective-permute-start.47) | collective-permute-done | bytes 524320 | tf_op jit(solution)/shard_map/ppermute | solution.py:336
  253.7 6.6 %collective-permute-done.45.rest_3_.rest_1_ = bf16[2,128,1024]{2,1,0:T(8,128)(2,1)} collective-permute-done((bf16[2,128,1024]{2,1,0:T(8,128)(2,1)}, bf16[2,128,1024]{2,1,0:T(8,128)(2,1)}, u32[]{:S(2)}, u32[]{:S(2)}) %collective-permute-start.45) | collective-permute-done | bytes 524320 | tf_op jit(solution)/shard_map/ppermute | solution.py:336
  264.6 6.8 %collective-permute-done.48.rest_5_.rest_3_ = bf16[2,128,1024]{2,1,0:T(8,128)(2,1)S(1)} collective-permute-done((bf16[2,128,1024]{2,1,0:T(8,128)(2,1)}, bf16[2,128,1024]{2,1,0:T(8,128)(2,1)S(1)}, u32[]{:S(2)}, u32[]{:S(2)}) %collective-permute-start.48) | collective-permute-done | bytes 524320 | tf_op jit(solution)/shard_map/ppermute | solution.py:336
  272.6 8.1 %shard_map.129 = bf16[2048,1024]{1,0:T(8,128)(2,1)} custom-call(s32[16,8]{1,0:T(8,128)S(1)} %copy.15.mask_ref.rest_0_, bf16[4,2,256,512]{3,2,1,0:T(8,128)(2,1)S(1)} %copy-done.1, bf16[256,1024]{1,0:T(8,128)(2,1)S(1)} %copy-done.5, bf16[256,1024]{1,0:T(8,128)(2,1)S(1)} %copy-done.40, bf16[256,1024]{1,0:T(8,128)(2,1)S(1)} %copy-done.36, ...), custom_call_target="tpu_custom_call" | custom-call | flops 4294967296 | bytes 10485760 | tf_op jit(solution)/shard_map/pallas_call | solution.py:69
  286.2 7.2 %collective-permute-done.42 = bf16[256,512]{1,0:T(8,128)(2,1)S(1)} collective-permute-done((bf16[256,512]{1,0:T(8,128)(2,1)S(1)}, bf16[256,512]{1,0:T(8,128)(2,1)S(1)}, u32[]{:S(2)}, u32[]{:S(2)}) %collective-permute-start.42) | collective-permute-done | bytes 262176 | tf_op jit(solution)/shard_map/ppermute | solution.py:325
  293.6 4.5 %collective-permute-start.44 = (bf16[256,512]{1,0:T(8,128)(2,1)S(1)}, bf16[256,512]{1,0:T(8,128)(2,1)S(1)}, u32[]{:S(2)}, u32[]{:S(2)}) collective-permute-start(bf16[256,512]{1,0:T(8,128)(2,1)S(1)} %fusion.4), channel_id=1, source_target_pairs={{0,0},{1,1},{10,2},{11,3},{20,4},{21,5},{30,6},{31,7},{2,8},{3,9},... | collective-permute-start | bytes 786440 | tf_op jit(solution)/shard_map/ppermute | solution.py:353
  300.4 9.4 %shard_map.128 = (bf16[4,128,512]{2,1,0:T(8,128)(2,1)S(1)}, bf16[4,128,512]{2,1,0:T(8,128)(2,1)S(1)}) custom-call(s32[1]{0:T(128)} %bitcast.place_ref, s32[8,16]{1,0:T(8,128)S(1)} %copy-done.49, s32[8,16]{1,0:T(8,128)S(1)} %copy-done.48, bf16[2,128,1024]{2,1,0:T(8,128)(2,1)} %pad_maximum_fusion.rest_2_.rest_0_, ...), custom_call_target="tpu_custom_call" | custom-call | flops 4294967296 | bytes 13631488 | tf_op jit(solution)/shard_map/pallas_call | solution.py:69
  313.3 7.7 %shard_map.130 = (bf16[4,128,512]{2,1,0:T(8,128)(2,1)S(1)}, bf16[4,128,512]{2,1,0:T(8,128)(2,1)S(1)}) custom-call(s32[1]{0:T(128)} %bitcast.place_ref, s32[8,16]{1,0:T(8,128)S(1)} %copy-done.49, s32[8,16]{1,0:T(8,128)S(1)} %copy-done.48, bf16[2,128,1024]{2,1,0:T(8,128)(2,1)S(1)} %pad_maximum_fusion.2.rest_2_.rest_8_, ...), custom_call_target="tpu_custom_call" | custom-call | flops 4294967296 | bytes 13631488 | tf_op jit(solution)/shard_map/pallas_call | solution.py:69
  322.2 5.6 %collective-permute-start.54 = (bf16[128,512]{1,0:T(8,128)(2,1)S(1)}, bf16[128,512]{1,0:T(8,128)(2,1)S(1)}, u32[]{:S(2)}, u32[]{:S(2)}) collective-permute-start(bf16[128,512]{1,0:T(8,128)(2,1)S(1)} %get-tuple-element.147), channel_id=1, source_target_pairs={{0,6},{1,7},{2,4},{3,5},{4,2},{5,3},{6,0},{7,1},{8,14},{9,15},{10,... | collective-permute-start | bytes 393224 | tf_op jit(solution)/shard_map/ppermute | solution.py:325
  327.9 7.2 %collective-permute-done.54 = bf16[128,512]{1,0:T(8,128)(2,1)S(1)} collective-permute-done((bf16[128,512]{1,0:T(8,128)(2,1)S(1)}, bf16[128,512]{1,0:T(8,128)(2,1)S(1)}, u32[]{:S(2)}, u32[]{:S(2)}) %collective-permute-start.54) | collective-permute-done | bytes 131104 | tf_op jit(solution)/shard_map/ppermute | solution.py:325
  335.1 4.6 %collective-permute-done.53 = bf16[128,512]{1,0:T(8,128)(2,1)S(1)} collective-permute-done((bf16[128,512]{1,0:T(8,128)(2,1)S(1)}, bf16[128,512]{1,0:T(8,128)(2,1)S(1)}, u32[]{:S(2)}, u32[]{:S(2)}) %collective-permute-start.53) | collective-permute-done | bytes 131104 | tf_op jit(solution)/shard_map/ppermute | solution.py:325
  348.1 8.6 %shard_map.132 = bf16[1024,2048]{1,0:T(8,128)(2,1)} custom-call(s32[8,16]{1,0:T(8,128)S(1)} %copy-done.48, bf16[4,2,256,512]{3,2,1,0:T(8,128)(2,1)S(1)} %shard_map.119.x_ref, bf16[2,128,1024]{2,1,0:T(8,128)(2,1)} %pad_maximum_fusion.rest_2_.rest_0_, bf16[2,128,1024]{2,1,0:T(8,128)(2,1)} %collective-permute-done.45.rest_3_.rest_1_, ...), custom_call_target="tpu_custom_call" | custom-call | flops 4294967296 | bytes 10485760 | tf_op jit(solution)/shard_map/pallas_call | solution.py:69
  358.9 5.7 %collective-permute-start.66 = (bf16[128,512]{1,0:T(8,128)(2,1)S(1)}, bf16[128,512]{1,0:T(8,128)(2,1)S(1)}, u32[]{:S(2)}, u32[]{:S(2)}) collective-permute-start(bf16[128,512]{1,0:T(8,128)(2,1)S(1)} %fusion.7), channel_id=1, source_target_pairs={{0,0},{1,1},{10,2},{11,3},{20,4},{21,5},{30,6},{31,7},{2,8},{3,9},... | collective-permute-start | bytes 393224 | tf_op jit(solution)/shard_map/ppermute | solution.py:353
  364.6 8.6 %shard_map.131 = bf16[1024,2048]{1,0:T(8,128)(2,1)} custom-call(s32[8,16]{1,0:T(8,128)S(1)} %copy-done.49, bf16[4,2,256,512]{3,2,1,0:T(8,128)(2,1)S(1)} %shard_map.119.x_ref, bf16[2,128,1024]{2,1,0:T(8,128)(2,1)} %pad_maximum_fusion.rest_2_.rest_0_, bf16[2,128,1024]{2,1,0:T(8,128)(2,1)} %collective-permute-done.45.rest_3_.rest_1_, ...), custom_call_target="tpu_custom_call" | custom-call | flops 4294967296 | bytes 10485760 | tf_op jit(solution)/shard_map/pallas_call | solution.py:69
  (259 shorter events, 129.7 us)
Async XLA Ops:
  15.3 24.6 %collective-permute-start.2 = (bf16[256,512]{1,0:T(8,128)(2,1)S(1)}, bf16[256,512]{1,0:T(8,128)(2,1)S(1)}, u32[]{:S(2)}, u32[]{:S(2)}) collective-permute-start(bf16[256,512]{1,0:T(8,128)(2,1)S(1)} %collective-permute-done.rest_0_), channel_id=1, source_target_pairs={{0,4},{1,5},{2,6},{3,7},{4,0},{5,1},{6,2},{7,3},{8,12},{9,13},{10,... | collective-permute-start | bytes 786440 | tf_op jit(solution)/shard_map/ppermute | solution.py:325
  51.7 24.6 %collective-permute-start.10 = (bf16[256,1024]{1,0:T(8,128)(2,1)S(1)}, bf16[256,1024]{1,0:T(8,128)(2,1)S(1)}, u32[]{:S(2)}, u32[]{:S(2)}) collective-permute-start(bf16[256,1024]{1,0:T(8,128)(2,1)S(1)} %get-tuple-element.75), channel_id=1, source_target_pairs={{0,16},{8,24},{16,0},{24,8},{1,17},{9,25},{17,1},{25,9},{2,18},{10... | collective-permute-start | bytes 1572872 | tf_op jit(solution)/shard_map/ppermute | solution.py:336
  71.0 24.9 %collective-permute-start.15 = (bf16[256,1024]{1,0:T(8,128)(2,1)S(1)}, bf16[256,1024]{1,0:T(8,128)(2,1)S(1)}, u32[]{:S(2)}, u32[]{:S(2)}) collective-permute-start(bf16[256,1024]{1,0:T(8,128)(2,1)S(1)} %get-tuple-element.88), channel_id=1, source_target_pairs={{0,16},{8,24},{16,0},{24,8},{1,17},{9,25},{17,1},{25,9},{2,18},{10... | collective-permute-start | bytes 1572872 | tf_op jit(solution)/shard_map/ppermute | solution.py:336
  76.2 29.5 %collective-permute-start.8 = (bf16[256,1024]{1,0:T(8,128)(2,1)S(1)}, bf16[256,1024]{1,0:T(8,128)(2,1)S(1)}, u32[]{:S(2)}, u32[]{:S(2)}) collective-permute-start(bf16[256,1024]{1,0:T(8,128)(2,1)S(1)} %get-tuple-element.72), channel_id=1, source_target_pairs={{0,8},{8,0},{16,24},{24,16},{1,9},{9,1},{17,25},{25,17},{2,10},{10... | collective-permute-start | bytes 1572872 | tf_op jit(solution)/shard_map/ppermute | solution.py:336
  79.2 24.5 %collective-permute-start.19 = (bf16[256,512]{1,0:T(8,128)(2,1)S(1)}, bf16[256,512]{1,0:T(8,128)(2,1)}, u32[]{:S(2)}, u32[]{:S(2)}) collective-permute-start(bf16[256,512]{1,0:T(8,128)(2,1)S(1)} %collective-permute-done.18.rest_0_), channel_id=1, source_target_pairs={{0,2},{1,3},{2,0},{3,1},{4,6},{5,7},{6,4},{7,5},{8,10},{9,11},{10,... | collective-permute-start | bytes 786440 | tf_op jit(solution)/shard_map/ppermute | solution.py:325
  84.2 22.7 %collective-permute-start.12 = (bf16[256,1024]{1,0:T(8,128)(2,1)S(1)}, bf16[256,1024]{1,0:T(8,128)(2,1)S(1)}, u32[]{:S(2)}, u32[]{:S(2)}) collective-permute-start(bf16[256,1024]{1,0:T(8,128)(2,1)S(1)} %add_convert_fusion.7), channel_id=1, source_target_pairs={{0,8},{8,0},{16,24},{24,16},{1,9},{9,1},{17,25},{25,17},{2,10},{10... | collective-permute-start | bytes 1572872 | tf_op jit(solution)/shard_map/ppermute | solution.py:336
  96.7 23.3 %collective-permute-start.11 = (bf16[256,1024]{1,0:T(8,128)(2,1)}, bf16[256,1024]{1,0:T(8,128)(2,1)}, u32[]{:S(2)}, u32[]{:S(2)}) collective-permute-start(bf16[256,1024]{1,0:T(8,128)(2,1)} %add_convert_fusion.8), channel_id=1, source_target_pairs={{0,16},{8,24},{16,0},{24,8},{1,17},{9,25},{17,1},{25,9},{2,18},{10... | collective-permute-start | bytes 1572872 | tf_op jit(solution)/shard_map/ppermute | solution.py:336
  103.7 20.5 %collective-permute-start.16 = (bf16[256,1024]{1,0:T(8,128)(2,1)}, bf16[256,1024]{1,0:T(8,128)(2,1)}, u32[]{:S(2)}, u32[]{:S(2)}) collective-permute-start(bf16[256,1024]{1,0:T(8,128)(2,1)} %get-tuple-element.89), channel_id=1, source_target_pairs={{0,16},{8,24},{16,0},{24,8},{1,17},{9,25},{17,1},{25,9},{2,18},{10... | collective-permute-start | bytes 1572872 | tf_op jit(solution)/shard_map/ppermute | solution.py:336
  112.5 23.6 %collective-permute-start.13 = (bf16[256,1024]{1,0:T(8,128)(2,1)}, bf16[256,1024]{1,0:T(8,128)(2,1)}, u32[]{:S(2)}, u32[]{:S(2)}) collective-permute-start(bf16[256,1024]{1,0:T(8,128)(2,1)} %get-tuple-element.83), channel_id=1, source_target_pairs={{0,8},{8,0},{16,24},{24,16},{1,9},{9,1},{17,25},{25,17},{2,10},{10... | collective-permute-start | bytes 1572872 | tf_op jit(solution)/shard_map/ppermute | solution.py:336
  120.1 21.9 %collective-permute-start.26 = (bf16[256,1024]{1,0:T(8,128)(2,1)}, bf16[256,1024]{1,0:T(8,128)(2,1)S(1)}, u32[]{:S(2)}, u32[]{:S(2)}) collective-permute-start(bf16[256,1024]{1,0:T(8,128)(2,1)} %copy-done.47), channel_id=1, source_target_pairs={{0,16},{8,24},{16,0},{24,8},{1,17},{9,25},{17,1},{25,9},{2,18},{10... | collective-permute-start | bytes 1572872 | tf_op jit(solution)/shard_map/ppermute | solution.py:336
  125.4 21.8 %collective-permute-start.33 = (bf16[256,1024]{1,0:T(8,128)(2,1)S(1)}, bf16[256,1024]{1,0:T(8,128)(2,1)S(1)}, u32[]{:S(2)}, u32[]{:S(2)}) collective-permute-start(bf16[256,1024]{1,0:T(8,128)(2,1)S(1)} %add_convert_fusion.4), channel_id=1, source_target_pairs={{0,8},{8,0},{16,24},{24,16},{1,9},{9,1},{17,25},{25,17},{2,10},{10... | collective-permute-start | bytes 1572872 | tf_op jit(solution)/shard_map/ppermute | solution.py:336
  136.1 22.4 %collective-permute-start.28 = (bf16[256,1024]{1,0:T(8,128)(2,1)S(1)}, bf16[256,1024]{1,0:T(8,128)(2,1)S(1)}, u32[]{:S(2)}, u32[]{:S(2)}) collective-permute-start(bf16[256,1024]{1,0:T(8,128)(2,1)S(1)} %get-tuple-element.98), channel_id=1, source_target_pairs={{0,8},{8,0},{16,24},{24,16},{1,9},{9,1},{17,25},{25,17},{2,10},{10... | collective-permute-start | bytes 1572872 | tf_op jit(solution)/shard_map/ppermute | solution.py:336
  143.5 24.6 %collective-permute-start.17 = (bf16[256,1024]{1,0:T(8,128)(2,1)S(1)}, bf16[256,1024]{1,0:T(8,128)(2,1)S(1)}, u32[]{:S(2)}, u32[]{:S(2)}) collective-permute-start(bf16[256,1024]{1,0:T(8,128)(2,1)S(1)} %add_convert_fusion.6), channel_id=1, source_target_pairs={{0,16},{8,24},{16,0},{24,8},{1,17},{9,25},{17,1},{25,9},{2,18},{10... | collective-permute-start | bytes 1572872 | tf_op jit(solution)/shard_map/ppermute | solution.py:336
  147.2 22.5 %collective-permute-start.34 = (bf16[256,1024]{1,0:T(8,128)(2,1)S(1)}, bf16[256,1024]{1,0:T(8,128)(2,1)S(1)}, u32[]{:S(2)}, u32[]{:S(2)}) collective-permute-start(bf16[256,1024]{1,0:T(8,128)(2,1)S(1)} %get-tuple-element.108), channel_id=1, source_target_pairs={{0,8},{8,0},{16,24},{24,16},{1,9},{9,1},{17,25},{25,17},{2,10},{10... | collective-permute-start | bytes 1572872 | tf_op jit(solution)/shard_map/ppermute | solution.py:336
  158.7 20.6 %collective-permute-start.37 = (bf16[256,1024]{1,0:T(8,128)(2,1)S(1)}, bf16[256,1024]{1,0:T(8,128)(2,1)S(1)}, u32[]{:S(2)}, u32[]{:S(2)}) collective-permute-start(bf16[256,1024]{1,0:T(8,128)(2,1)S(1)} %add_convert_fusion.3), channel_id=1, source_target_pairs={{0,16},{8,24},{16,0},{24,8},{1,17},{9,25},{17,1},{25,9},{2,18},{10... | collective-permute-start | bytes 1572872 | tf_op jit(solution)/shard_map/ppermute | solution.py:336
  189.8 25.5 %collective-permute-start.30 = (bf16[256,1024]{1,0:T(8,128)(2,1)S(1)}, bf16[256,1024]{1,0:T(8,128)(2,1)S(1)}, u32[]{:S(2)}, u32[]{:S(2)}) collective-permute-start(bf16[256,1024]{1,0:T(8,128)(2,1)S(1)} %get-tuple-element.103.rest_1_.rest_0_), channel_id=1, source_target_pairs={{0,8},{8,0},{16,24},{24,16},{1,9},{9,1},{17,25},{25,17},{2,10},{10... | collective-permute-start | bytes 1572872 | tf_op jit(solution)/shard_map/ppermute | solution.py:336
  191.3 24.0 %collective-permute-start.38 = (bf16[256,1024]{1,0:T(8,128)(2,1)S(1)}, bf16[256,1024]{1,0:T(8,128)(2,1)S(1)}, u32[]{:S(2)}, u32[]{:S(2)}) collective-permute-start(bf16[256,1024]{1,0:T(8,128)(2,1)S(1)} %get-tuple-element.113.rest_5_.rest_4_), channel_id=1, source_target_pairs={{0,16},{8,24},{16,0},{24,8},{1,17},{9,25},{17,1},{25,9},{2,18},{10... | collective-permute-start | bytes 1572872 | tf_op jit(solution)/shard_map/ppermute | solution.py:336
  231.3 31.7 %collective-permute-start.40 = (bf16[4,256,512]{2,1,0:T(8,128)(2,1)}, bf16[4,256,512]{2,1,0:T(8,128)(2,1)}, u32[]{:S(2)}, u32[]{:S(2)}) collective-permute-start(bf16[4,256,512]{2,1,0:T(8,128)(2,1)} %get-tuple-element.116), channel_id=1, source_target_pairs={{0,1},{1,0},{2,3},{3,2},{4,5},{5,4},{6,7},{7,6},{8,9},{9,8},{10,11... | collective-permute-start | bytes 3145736 | tf_op jit(solution)/shard_map/ppermute | solution.py:325
  236.6 23.7 %collective-permute-start.45 = (bf16[2,128,1024]{2,1,0:T(8,128)(2,1)}, bf16[2,128,1024]{2,1,0:T(8,128)(2,1)}, u32[]{:S(2)}, u32[]{:S(2)}) collective-permute-start(bf16[2,128,1024]{2,1,0:T(8,128)(2,1)} %pad_maximum_fusion.rest_2_.rest_0_), channel_id=1, source_target_pairs={{0,8},{8,0},{16,24},{24,16},{1,9},{9,1},{17,25},{25,17},{2,10},{10... | collective-permute-start | bytes 1572872 | tf_op jit(solution)/shard_map/ppermute | solution.py:336
  237.5 23.9 %collective-permute-start.49 = (bf16[2,128,1024]{2,1,0:T(8,128)(2,1)}, bf16[2,128,1024]{2,1,0:T(8,128)(2,1)}, u32[]{:S(2)}, u32[]{:S(2)}) collective-permute-start(bf16[2,128,1024]{2,1,0:T(8,128)(2,1)} %pad_maximum_fusion.1.rest_6_.rest_4_), channel_id=1, source_target_pairs={{0,16},{8,24},{16,0},{24,8},{1,17},{9,25},{17,1},{25,9},{2,18},{10... | collective-permute-start | bytes 1572872 | tf_op jit(solution)/shard_map/ppermute | solution.py:336
  250.1 21.3 %collective-permute-start.48 = (bf16[2,128,1024]{2,1,0:T(8,128)(2,1)}, bf16[2,128,1024]{2,1,0:T(8,128)(2,1)S(1)}, u32[]{:S(2)}, u32[]{:S(2)}) collective-permute-start(bf16[2,128,1024]{2,1,0:T(8,128)(2,1)} %collective-permute-done.46.rest_4_.rest_2_), channel_id=1, source_target_pairs={{0,8},{8,0},{16,24},{24,16},{1,9},{9,1},{17,25},{25,17},{2,10},{10... | collective-permute-start | bytes 1572872 | tf_op jit(solution)/shard_map/ppermute | solution.py:336
  251.1 21.4 %collective-permute-start.50 = (bf16[2,128,1024]{2,1,0:T(8,128)(2,1)}, bf16[2,128,1024]{2,1,0:T(8,128)(2,1)S(1)}, u32[]{:S(2)}, u32[]{:S(2)}) collective-permute-start(bf16[2,128,1024]{2,1,0:T(8,128)(2,1)} %collective-permute-done.47.rest_7_.rest_5_), channel_id=1, source_target_pairs={{0,16},{8,24},{16,0},{24,8},{1,17},{9,25},{17,1},{25,9},{2,18},{10... | collective-permute-start | bytes 1572872 | tf_op jit(solution)/shard_map/ppermute | solution.py:336
  260.3 21.9 %collective-permute-start.58 = (bf16[2,128,1024]{2,1,0:T(8,128)(2,1)S(1)}, bf16[2,128,1024]{2,1,0:T(8,128)(2,1)S(1)}, u32[]{:S(2)}, u32[]{:S(2)}) collective-permute-start(bf16[2,128,1024]{2,1,0:T(8,128)(2,1)S(1)} %pad_maximum_fusion.3.rest_6_.rest_12_), channel_id=1, source_target_pairs={{0,8},{8,0},{16,24},{24,16},{1,9},{9,1},{17,25},{25,17},{2,10},{10... | collective-permute-start | bytes 1572872 | tf_op jit(solution)/shard_map/ppermute | solution.py:336
  261.4 21.9 %collective-permute-start.57 = (bf16[2,128,1024]{2,1,0:T(8,128)(2,1)S(1)}, bf16[2,128,1024]{2,1,0:T(8,128)(2,1)S(1)}, u32[]{:S(2)}, u32[]{:S(2)}) collective-permute-start(bf16[2,128,1024]{2,1,0:T(8,128)(2,1)S(1)} %pad_maximum_fusion.2.rest_2_.rest_8_), channel_id=1, source_target_pairs={{0,16},{8,24},{16,0},{24,8},{1,17},{9,25},{17,1},{25,9},{2,18},{10... | collective-permute-start | bytes 1572872 | tf_op jit(solution)/shard_map/ppermute | solution.py:336
  264.5 20.3 %collective-permute-start.41 = (bf16[256,512]{1,0:T(8,128)(2,1)S(1)}, bf16[256,512]{1,0:T(8,128)(2,1)S(1)}, u32[]{:S(2)}, u32[]{:S(2)}) collective-permute-start(bf16[256,512]{1,0:T(8,128)(2,1)S(1)} %get-tuple-element.143), channel_id=1, source_target_pairs={{0,2},{1,3},{2,0},{3,1},{4,6},{5,7},{6,4},{7,5},{8,10},{9,11},{10,... | collective-permute-start | bytes 786440 | tf_op jit(solution)/shard_map/ppermute | solution.py:325
  272.5 21.0 %collective-permute-start.42 = (bf16[256,512]{1,0:T(8,128)(2,1)S(1)}, bf16[256,512]{1,0:T(8,128)(2,1)S(1)}, u32[]{:S(2)}, u32[]{:S(2)}) collective-permute-start(bf16[256,512]{1,0:T(8,128)(2,1)S(1)} %get-tuple-element.145), channel_id=1, source_target_pairs={{0,4},{1,5},{2,6},{3,7},{4,0},{5,1},{6,2},{7,3},{8,12},{9,13},{10,... | collective-permute-start | bytes 786440 | tf_op jit(solution)/shard_map/ppermute | solution.py:325
  282.2 27.7 %collective-permute-start.56 = (bf16[2,128,1024]{2,1,0:T(8,128)(2,1)S(1)}, bf16[2,128,1024]{2,1,0:T(8,128)(2,1)S(1)}, u32[]{:S(2)}, u32[]{:S(2)}) collective-permute-start(bf16[2,128,1024]{2,1,0:T(8,128)(2,1)S(1)} %pad_maximum_fusion.2.rest_2_.rest_8_), channel_id=1, source_target_pairs={{0,8},{8,0},{16,24},{24,16},{1,9},{9,1},{17,25},{25,17},{2,10},{10... | collective-permute-start | bytes 1572872 | tf_op jit(solution)/shard_map/ppermute | solution.py:336
  283.3 26.6 %collective-permute-start.60 = (bf16[2,128,1024]{2,1,0:T(8,128)(2,1)S(1)}, bf16[2,128,1024]{2,1,0:T(8,128)(2,1)S(1)}, u32[]{:S(2)}, u32[]{:S(2)}) collective-permute-start(bf16[2,128,1024]{2,1,0:T(8,128)(2,1)S(1)} %pad_maximum_fusion.3.rest_6_.rest_12_), channel_id=1, source_target_pairs={{0,16},{8,24},{16,0},{24,8},{1,17},{9,25},{17,1},{25,9},{2,18},{10... | collective-permute-start | bytes 1572872 | tf_op jit(solution)/shard_map/ppermute | solution.py:336
  284.8 25.1 %collective-permute-start.59 = (bf16[2,128,1024]{2,1,0:T(8,128)(2,1)S(1)}, bf16[2,128,1024]{2,1,0:T(8,128)(2,1)S(1)}, u32[]{:S(2)}, u32[]{:S(2)}) collective-permute-start(bf16[2,128,1024]{2,1,0:T(8,128)(2,1)S(1)} %collective-permute-done.57.rest_4_.rest_10_), channel_id=1, source_target_pairs={{0,8},{8,0},{16,24},{24,16},{1,9},{9,1},{17,25},{25,17},{2,10},{10... | collective-permute-start | bytes 1572872 | tf_op jit(solution)/shard_map/ppermute | solution.py:336
  285.7 27.6 %collective-permute-start.61 = (bf16[2,128,1024]{2,1,0:T(8,128)(2,1)S(1)}, bf16[2,128,1024]{2,1,0:T(8,128)(2,1)S(1)}, u32[]{:S(2)}, u32[]{:S(2)}) collective-permute-start(bf16[2,128,1024]{2,1,0:T(8,128)(2,1)S(1)} %collective-permute-done.58.rest_7_.rest_13_), channel_id=1, source_target_pairs={{0,16},{8,24},{16,0},{24,8},{1,17},{9,25},{17,1},{25,9},{2,18},{10... | collective-permute-start | bytes 1572872 | tf_op jit(solution)/shard_map/ppermute | solution.py:336
  321.0 22.7 %collective-permute-start.62 = (bf16[4,128,512]{2,1,0:T(8,128)(2,1)S(1)}, bf16[4,128,512]{2,1,0:T(8,128)(2,1)S(1)}, u32[]{:S(2)}, u32[]{:S(2)}) collective-permute-start(bf16[4,128,512]{2,1,0:T(8,128)(2,1)S(1)} %get-tuple-element.135), channel_id=1, source_target_pairs={{0,1},{1,0},{2,3},{3,2},{4,5},{5,4},{6,7},{7,6},{8,9},{9,8},{10,11... | collective-permute-start | bytes 1572872 | tf_op jit(solution)/shard_map/ppermute | solution.py:325
  339.8 33.4 %collective-permute-start.55 = (bf16[128,512]{1,0:T(8,128)(2,1)S(1)}, bf16[128,512]{1,0:T(8,128)(2,1)S(1)}, u32[]{:S(2)}, u32[]{:S(2)}) collective-permute-start(bf16[128,512]{1,0:T(8,128)(2,1)S(1)} %fusion.10), channel_id=1, source_target_pairs={{0,0},{1,1},{10,2},{11,3},{20,4},{21,5},{30,6},{31,7},{2,8},{3,9},... | collective-permute-start | bytes 393224 | tf_op jit(solution)/shard_map/ppermute | solution.py:353
  (93 other events, 1393.6 us)
where the time goes:
time: 375 us
  waiting for transfers between devices  152 us (41%)
  starting transfers between devices  107 us (29%)
  Pallas kernels  77.7 us (21%)
  local copies, waits for them, and re-layouts  21.8 us (6%)
  other arithmetic  14.6 us (4%)
    ppermute x36, waiting for transfers between devices, over_dp(): lax.ppermute(value, 'dp', [(i, i ^ 1 << bit) for i in range(dp)])  103 us
    pallas_call x14, Pallas kernels, call(): pl.pallas_call(kernel, grid_spec=pltpu.PrefetchScalarGridSpec(num_scalar_...  77.7 us
    ppermute x36, starting transfers between devices, over_dp(): lax.ppermute(value, 'dp', [(i, i ^ 1 << bit) for i in range(dp)])  46.5 us
    ppermute x26, waiting for transfers between devices, over_mp(): return lax.ppermute(value, 'mp', [(j, j ^ step) for j in range(mp)])  42.7 us
    ppermute x26, starting transfers between devices, over_mp(): return lax.ppermute(value, 'mp', [(j, j ^ step) for j in range(mp)])  33.7 us
    unnamed x118, local copies, waits for them, and re-layouts  20 us
    ppermute x3, starting transfers between devices, collect_rows(): return lax.ppermute(own.astype(bf16), ('dp', 'mp'), back)  14.2 us
  transfers between devices with their start and end apart: 67, of which 27 were waited for; matrix products, arithmetic and copies ran while one was open for 4% of the time, Pallas kernels for 17%

commit v1 on v0

--- a/solution.py
+++ b/solution.py
@@ -382,7 +382,9 @@
     tok, tok_line = spread_rows(tok_moved)
     gate_parts = [project(tok, gate_weight, gate_mask, h, False) for h in colors]
     tok_up = after(tok, *[p[0] for p in gate_parts])
-    up_parts = [project(tok_up, up_weight, up_mask, h, False) for h in colors]
+    up_parts = []
+    for h in colors:
+        up_parts.append(project(tok_up, up_weight, up_mask, h, False))
     cot, _ = spread_rows(after(cot_moved, *tok_line, up_parts[0][0]))
     grad_parts = [project(cot, down_weight, down_mask, h, True) for h in colors]
     gate_pre = reduce_dp(gate_parts)
@@ -421,7 +423,7 @@
         )
         token_grad.append(collect_rows(part))
         deltas += delta
-        done = (layer_out, part[0])
+        done = (part[0],)
     last_tok = after(tok, part[0])
     gate_grad = outer_up(last_tok, deltas, 0, CHUNKS, gate_mask, scale)
     up_grad = outer_up(last_tok, deltas, 1, CHUNKS, up_mask, scale)

time: 375 us -> 405 us (1.080); the launches traced: 375 us -> 399 us
  local copies, waits for them, and re-layouts: 21.8 us -> 35.7 us
  waiting for transfers between devices: 152 us -> 157 us
    unnamed x118 -> x178, local copies, waits for them, and re-layouts: 20 us -> 34.6 us
    ppermute x36, waiting for transfers between devices: 103 us -> 109 us  [over_dp(): lax.ppermute(value, 'dp', [(i, i ^ 1 << bit) for i in range(dp)])]
    ppermute x3, starting transfers between devices: 14.2 us -> 20.5 us  [collect_rows(): return lax.ppermute(own.astype(bf16), ('dp', 'mp'), back)]
  transfers between devices with their start and end apart: 67 -> 67, of which waited for: 27 -> 25; matrix products, arithmetic and copies ran while one was open for 4% -> 4% of each run, Pallas kernels for 17% -> 19%
where the time goes in v1:
time: 405 us; the launch traced here: 399 us
  waiting for transfers between devices  157 us (39%)
  starting transfers between devices  110 us (27%)
  Pallas kernels  78.4 us (19%)
  local copies, waits for them, and re-layouts  35.7 us (9%)
  other arithmetic  16.9 us (4%)
    ppermute x36, waiting for transfers between devices, over_dp(): lax.ppermute(value, 'dp', [(i, i ^ 1 << bit) for i in range(dp)])  109 us
    pallas_call x14, Pallas kernels, call(): pl.pallas_call(kernel, grid_spec=pltpu.PrefetchScalarGridSpec(num_scalar_...  78.4 us
    ppermute x36, starting transfers between devices, over_dp(): lax.ppermute(value, 'dp', [(i, i ^ 1 << bit) for i in range(dp)])  46.4 us
    ppermute x26, waiting for transfers between devices, over_mp(): return lax.ppermute(value, 'mp', [(j, j ^ step) for j in range(mp)])  40.7 us
    unnamed x178, local copies, waits for them, and re-layouts  34.6 us
    ppermute x26, starting transfers between devices, over_mp(): return lax.ppermute(value, 'mp', [(j, j ^ step) for j in range(mp)])  30.1 us
    ppermute x3, starting transfers between devices, collect_rows(): return lax.ppermute(own.astype(bf16), ('dp', 'mp'), back)  20.5 us
  transfers between devices with their start and end apart: 67, of which 25 were waited for; matrix products, arithmetic and copies ran while one was open for 4% of the time, Pallas kernels for 19%

profile of v1, /device:TPU:6, one launch (start us, length us, event | category | flops | bytes accessed | tf_op | source)
XLA Modules:
  0.0 398.7 jit_solution(10398738982044166446)
XLA Ops:
  0.6 5.4 %collective-permute-start = (bf16[256,512]{1,0:T(8,128)(2,1)}, bf16[256,512]{1,0:T(8,128)(2,1)S(1)}, u32[]{:S(2)}, u32[]{:S(2)}) collective-permute-start(bf16[256,512]{1,0:T(8,128)(2,1)} %param.8), channel_id=1, source_target_pairs={{0,0},{1,1},{2,10},{3,11},{4,20},{5,21},{6,30},{7,31},{8,2},{9,3},... | collective-permute-start | bytes 786440 | tf_op jit(solution)/shard_map/ppermute | solution.py:380
  6.1 6.7 %collective-permute-done.rest_0_ = bf16[256,512]{1,0:T(8,128)(2,1)S(1)} collective-permute-done((bf16[256,512]{1,0:T(8,128)(2,1)}, bf16[256,512]{1,0:T(8,128)(2,1)S(1)}, u32[]{:S(2)}, u32[]{:S(2)}) %collective-permute-start) | collective-permute-done | bytes 262176 | tf_op jit(solution)/shard_map/ppermute | solution.py:380
  15.3 12.8 %collective-permute-start.2 = (bf16[256,512]{1,0:T(8,128)(2,1)S(1)}, bf16[256,512]{1,0:T(8,128)(2,1)S(1)}, u32[]{:S(2)}, u32[]{:S(2)}) collective-permute-start(bf16[256,512]{1,0:T(8,128)(2,1)S(1)} %collective-permute-done.rest_0_), channel_id=1, source_target_pairs={{0,4},{1,5},{2,6},{3,7},{4,0},{5,1},{6,2},{7,3},{8,12},{9,13},{10,... | collective-permute-start | bytes 786440 | tf_op jit(solution)/shard_map/ppermute | solution.py:325
  28.6 11.3 %collective-permute-done.2.rest_2_ = bf16[256,512]{1,0:T(8,128)(2,1)S(1)} collective-permute-done((bf16[256,512]{1,0:T(8,128)(2,1)S(1)}, bf16[256,512]{1,0:T(8,128)(2,1)S(1)}, u32[]{:S(2)}, u32[]{:S(2)}) %collective-permute-start.2) | collective-permute-done | bytes 262176 | tf_op jit(solution)/shard_map/ppermute | solution.py:325
  54.6 7.1 %collective-permute-start.18 = (bf16[256,512]{1,0:T(8,128)(2,1)S(1)}, bf16[256,512]{1,0:T(8,128)(2,1)S(1)}, u32[]{:S(2)}, u32[]{:S(2)}) collective-permute-start(bf16[256,512]{1,0:T(8,128)(2,1)S(1)} %copy-done.87), channel_id=1, source_target_pairs={{0,0},{1,1},{2,10},{3,11},{4,20},{5,21},{6,30},{7,31},{8,2},{9,3},... | collective-permute-start | bytes 786440 | tf_op jit(solution)/shard_map/ppermute | solution.py:381
  65.6 4.5 %shard_map.122 = (bf16[256,1024]{1,0:T(8,128)(2,1)S(1)}, bf16[256,1024]{1,0:T(8,128)(2,1)}, bf16[256,1024]{1,0:T(8,128)(2,1)S(1)}, bf16[256,1024]{1,0:T(8,128)(2,1)}) custom-call(s32[8,16]{1,0:T(8,128)S(1)} %copy-done.76, bf16[4,2,256,512]{3,2,1,0:T(8,128)(2,1)S(1)} %shard_map.119.x_ref, bf16[1024,2048]{1,0:T(8,128)(2,1)S(1)} %copy-done.40), custom_call_target="tpu_custom_call" | custom-call | flops 2147483648 | bytes 6291456 | tf_op jit(solution)/shard_map/pallas_call | solution.py:69
  71.0 5.2 %collective-permute-start.15 = (bf16[256,1024]{1,0:T(8,128)(2,1)S(1)}, bf16[256,1024]{1,0:T(8,128)(2,1)S(1)}, u32[]{:S(2)}, u32[]{:S(2)}) collective-permute-start(bf16[256,1024]{1,0:T(8,128)(2,1)S(1)} %get-tuple-element.88), channel_id=1, source_target_pairs={{0,16},{8,24},{16,0},{24,8},{1,17},{9,25},{17,1},{25,9},{2,18},{10... | collective-permute-start | bytes 1572872 | tf_op jit(solution)/shard_map/ppermute | solution.py:336
  79.2 5.0 %collective-permute-start.19 = (bf16[256,512]{1,0:T(8,128)(2,1)S(1)}, bf16[256,512]{1,0:T(8,128)(2,1)}, u32[]{:S(2)}, u32[]{:S(2)}) collective-permute-start(bf16[256,512]{1,0:T(8,128)(2,1)S(1)} %collective-permute-done.18.rest_0_), channel_id=1, source_target_pairs={{0,2},{1,3},{2,0},{3,1},{4,6},{5,7},{6,4},{7,5},{8,10},{9,11},{10,... | collective-permute-start | bytes 786440 | tf_op jit(solution)/shard_map/ppermute | solution.py:325
  85.9 10.0 %collective-permute-done.20.rest_2_ = bf16[256,512]{1,0:T(8,128)(2,1)S(1)} collective-permute-done((bf16[256,512]{1,0:T(8,128)(2,1)S(1)}, bf16[256,512]{1,0:T(8,128)(2,1)S(1)}, u32[]{:S(2)}, u32[]{:S(2)}) %collective-permute-start.20) | collective-permute-done | bytes 262176 | tf_op jit(solution)/shard_map/ppermute | solution.py:325
  106.9 4.8 %collective-permute-start.14 = (bf16[256,1024]{1,0:T(8,128)(2,1)}, bf16[256,1024]{1,0:T(8,128)(2,1)}, u32[]{:S(2)}, u32[]{:S(2)}) collective-permute-start(bf16[256,1024]{1,0:T(8,128)(2,1)} %get-tuple-element.86), channel_id=1, source_target_pairs={{0,8},{8,0},{16,24},{24,16},{1,9},{9,1},{17,25},{25,17},{2,10},{10... | collective-permute-start | bytes 1572872 | tf_op jit(solution)/shard_map/ppermute | solution.py:336
  129.2 6.8 %collective-permute-done.13 = bf16[256,1024]{1,0:T(8,128)(2,1)} collective-permute-done((bf16[256,1024]{1,0:T(8,128)(2,1)}, bf16[256,1024]{1,0:T(8,128)(2,1)}, u32[]{:S(2)}, u32[]{:S(2)}) %collective-permute-start.13) | collective-permute-done | bytes 524320 | tf_op jit(solution)/shard_map/ppermute | solution.py:336
  149.2 9.2 %collective-permute-done.28 = bf16[256,1024]{1,0:T(8,128)(2,1)S(1)} collective-permute-done((bf16[256,1024]{1,0:T(8,128)(2,1)S(1)}, bf16[256,1024]{1,0:T(8,128)(2,1)S(1)}, u32[]{:S(2)}, u32[]{:S(2)}) %collective-permute-start.28) | collective-permute-done | bytes 524320 | tf_op jit(solution)/shard_map/ppermute | solution.py:336
  158.8 9.3 %collective-permute-done.17 = bf16[256,1024]{1,0:T(8,128)(2,1)S(1)} collective-permute-done((bf16[256,1024]{1,0:T(8,128)(2,1)S(1)}, bf16[256,1024]{1,0:T(8,128)(2,1)S(1)}, u32[]{:S(2)}, u32[]{:S(2)}) %collective-permute-start.17) | collective-permute-done | bytes 524320 | tf_op jit(solution)/shard_map/ppermute | solution.py:336
  169.6 9.7 %collective-permute-done.37 = bf16[256,1024]{1,0:T(8,128)(2,1)S(1)} collective-permute-done((bf16[256,1024]{1,0:T(8,128)(2,1)S(1)}, bf16[256,1024]{1,0:T(8,128)(2,1)S(1)}, u32[]{:S(2)}, u32[]{:S(2)}) %collective-permute-start.37) | collective-permute-done | bytes 524320 | tf_op jit(solution)/shard_map/ppermute | solution.py:336
  181.7 6.1 %collective-permute-done.31 = bf16[256,1024]{1,0:T(8,128)(2,1)S(1)} collective-permute-done((bf16[256,1024]{1,0:T(8,128)(2,1)S(1)}, bf16[256,1024]{1,0:T(8,128)(2,1)S(1)}, u32[]{:S(2)}, u32[]{:S(2)}) %collective-permute-start.31) | collective-permute-done | bytes 524320 | tf_op jit(solution)/shard_map/ppermute | solution.py:336
  193.5 10.5 %collective-permute-done.30.rest_2_.rest_1_ = bf16[256,1024]{1,0:T(8,128)(2,1)S(1)} collective-permute-done((bf16[256,1024]{1,0:T(8,128)(2,1)S(1)}, bf16[256,1024]{1,0:T(8,128)(2,1)S(1)}, u32[]{:S(2)}, u32[]{:S(2)}) %collective-permute-start.30) | collective-permute-done | bytes 524320 | tf_op jit(solution)/shard_map/ppermute | solution.py:336
  204.1 8.5 %collective-permute-done.35.rest_6_.rest_5_ = bf16[256,1024]{1,0:T(8,128)(2,1)S(1)} collective-permute-done((bf16[256,1024]{1,0:T(8,128)(2,1)S(1)}, bf16[256,1024]{1,0:T(8,128)(2,1)S(1)}, u32[]{:S(2)}, u32[]{:S(2)}) %collective-permute-start.35) | collective-permute-done | bytes 524320 | tf_op jit(solution)/shard_map/ppermute | solution.py:336
  217.5 9.9 %collective-permute-done.36.rest_4_.rest_3_ = bf16[256,1024]{1,0:T(8,128)(2,1)S(1)} collective-permute-done((bf16[256,1024]{1,0:T(8,128)(2,1)S(1)}, bf16[256,1024]{1,0:T(8,128)(2,1)S(1)}, u32[]{:S(2)}, u32[]{:S(2)}) %collective-permute-start.36) | collective-permute-done | bytes 524320 | tf_op jit(solution)/shard_map/ppermute | solution.py:336
  229.7 8.9 %collective-permute-done.47.rest_7_.rest_5_ = bf16[2,128,1024]{2,1,0:T(8,128)(2,1)S(1)} collective-permute-done((bf16[2,128,1024]{2,1,0:T(8,128)(2,1)S(1)}, bf16[2,128,1024]{2,1,0:T(8,128)(2,1)S(1)}, u32[]{:S(2)}, u32[]{:S(2)}) %collective-permute-start.47) | collective-permute-done | bytes 524320 | tf_op jit(solution)/shard_map/ppermute | solution.py:336
  243.3 8.5 %shard_map.127 = (bf16[4,256,512]{2,1,0:T(8,128)(2,1)S(1)}, bf16[4,256,512]{2,1,0:T(8,128)(2,1)}) custom-call(s32[1]{0:T(128)} %bitcast.place_ref, s32[16,8]{1,0:T(8,128)S(1)} %copy.15.mask_ref.rest_0_, bf16[256,1024]{1,0:T(8,128)(2,1)S(1)} %get-tuple-element.103.rest_1_.rest_0_, bf16[256,1024]{1,0:T(8,128)(2,1)S(1)} %collective-permute-done.30.rest_2_.rest_1_, ...), custom_call_target="tpu_custom_call" | custom-call | flops 4294967296 | bytes 10485760 | tf_op jit(solution)/shard_map/pallas_call | solution.py:69
  252.8 4.8 %collective-permute-done.48.rest_5_.rest_3_ = bf16[2,128,1024]{2,1,0:T(8,128)(2,1)S(1)} collective-permute-done((bf16[2,128,1024]{2,1,0:T(8,128)(2,1)S(1)}, bf16[2,128,1024]{2,1,0:T(8,128)(2,1)S(1)}, u32[]{:S(2)}, u32[]{:S(2)}) %collective-permute-start.48) | collective-permute-done | bytes 524320 | tf_op jit(solution)/shard_map/ppermute | solution.py:336
  260.2 8.4 %shard_map.128 = (bf16[4,128,512]{2,1,0:T(8,128)(2,1)S(1)}, bf16[4,128,512]{2,1,0:T(8,128)(2,1)}) custom-call(s32[1]{0:T(128)} %bitcast.place_ref, s32[8,16]{1,0:T(8,128)S(1)} %copy-done.77, s32[8,16]{1,0:T(8,128)S(1)} %copy-done.76, bf16[2,128,1024]{2,1,0:T(8,128)(2,1)S(1)} %pad_maximum_fusion.rest_2_.rest_0_, ...), custom_call_target="tpu_custom_call" | custom-call | flops 4294967296 | bytes 13631488 | tf_op jit(solution)/shard_map/pallas_call | solution.py:69
  279.3 8.1 %shard_map.129 = bf16[2048,1024]{1,0:T(8,128)(2,1)} custom-call(s32[16,8]{1,0:T(8,128)S(1)} %copy.15.mask_ref.rest_0_, bf16[4,2,256,512]{3,2,1,0:T(8,128)(2,1)S(1)} %copy-done.1, bf16[256,1024]{1,0:T(8,128)(2,1)S(1)} %copy-done.5, bf16[256,1024]{1,0:T(8,128)(2,1)S(1)} %copy-done.66, bf16[256,1024]{1,0:T(8,128)(2,1)S(1)} %copy-done.64, ...), custom_call_target="tpu_custom_call" | custom-call | flops 4294967296 | bytes 10485760 | tf_op jit(solution)/shard_map/pallas_call | solution.py:69
  295.8 6.7 %collective-permute-done.56.rest_3_.rest_9_ = bf16[2,128,1024]{2,1,0:T(8,128)(2,1)S(1)} collective-permute-done((bf16[2,128,1024]{2,1,0:T(8,128)(2,1)}, bf16[2,128,1024]{2,1,0:T(8,128)(2,1)S(1)}, u32[]{:S(2)}, u32[]{:S(2)}) %collective-permute-start.56) | collective-permute-done | bytes 524320 | tf_op jit(solution)/shard_map/ppermute | solution.py:336
  304.9 8.5 %collective-permute-done.59.rest_5_.rest_11_ = bf16[2,128,1024]{2,1,0:T(8,128)(2,1)S(1)} collective-permute-done((bf16[2,128,1024]{2,1,0:T(8,128)(2,1)}, bf16[2,128,1024]{2,1,0:T(8,128)(2,1)S(1)}, u32[]{:S(2)}, u32[]{:S(2)}) %collective-permute-start.59) | collective-permute-done | bytes 524320 | tf_op jit(solution)/shard_map/ppermute | solution.py:336
  315.7 9.5 %shard_map.130 = (bf16[4,128,512]{2,1,0:T(8,128)(2,1)S(1)}, bf16[4,128,512]{2,1,0:T(8,128)(2,1)}) custom-call(s32[1]{0:T(128)} %bitcast.place_ref, s32[8,16]{1,0:T(8,128)S(1)} %copy-done.77, s32[8,16]{1,0:T(8,128)S(1)} %copy-done.76, bf16[2,128,1024]{2,1,0:T(8,128)(2,1)} %pad_maximum_fusion.2.rest_2_.rest_8_, ...), custom_call_target="tpu_custom_call" | custom-call | flops 4294967296 | bytes 13631488 | tf_op jit(solution)/shard_map/pallas_call | solution.py:69
  334.1 6.6 %collective-permute-done.41 = bf16[256,512]{1,0:T(8,128)(2,1)S(1)} collective-permute-done((bf16[256,512]{1,0:T(8,128)(2,1)}, bf16[256,512]{1,0:T(8,128)(2,1)S(1)}, u32[]{:S(2)}, u32[]{:S(2)}) %collective-permute-start.41) | collective-permute-done | bytes 262176 | tf_op jit(solution)/shard_map/ppermute | solution.py:325
  340.7 12.5 %collective-permute-done.42 = bf16[256,512]{1,0:T(8,128)(2,1)} collective-permute-done((bf16[256,512]{1,0:T(8,128)(2,1)}, bf16[256,512]{1,0:T(8,128)(2,1)}, u32[]{:S(2)}, u32[]{:S(2)}) %collective-permute-start.42) | collective-permute-done | bytes 262176 | tf_op jit(solution)/shard_map/ppermute | solution.py:325
  354.5 6.4 %collective-permute-start.44 = (bf16[256,512]{1,0:T(8,128)(2,1)S(1)}, bf16[256,512]{1,0:T(8,128)(2,1)S(1)}, u32[]{:S(2)}, u32[]{:S(2)}) collective-permute-start(bf16[256,512]{1,0:T(8,128)(2,1)S(1)} %fusion.4), channel_id=1, source_target_pairs={{0,0},{1,1},{10,2},{11,3},{20,4},{21,5},{30,6},{31,7},{2,8},{3,9},... | collective-permute-start | bytes 786440 | tf_op jit(solution)/shard_map/ppermute | solution.py:353
  368.9 8.6 %shard_map.132 = bf16[1024,2048]{1,0:T(8,128)(2,1)} custom-call(s32[8,16]{1,0:T(8,128)S(1)} %copy-done.76, bf16[4,2,256,512]{3,2,1,0:T(8,128)(2,1)S(1)} %shard_map.119.x_ref, bf16[2,128,1024]{2,1,0:T(8,128)(2,1)S(1)} %copy-done.17, bf16[2,128,1024]{2,1,0:T(8,128)(2,1)S(1)} %copy-done.48, bf16[2,128,1024]{2,1,0:T(8,128)(2,1)S(1)} %copy-done.46, ...), custom_call_target="tpu_custom_call" | custom-call | flops 4294967296 | bytes 10485760 | tf_op jit(solution)/shard_map/pallas_call | solution.py:69
  377.6 11.1 %collective-permute-start.66 = (bf16[128,512]{1,0:T(8,128)(2,1)S(1)}, bf16[128,512]{1,0:T(8,128)(2,1)S(1)}, u32[]{:S(2)}, u32[]{:S(2)}) collective-permute-start(bf16[128,512]{1,0:T(8,128)(2,1)S(1)} %fusion.7), channel_id=1, source_target_pairs={{0,0},{1,1},{10,2},{11,3},{20,4},{21,5},{30,6},{31,7},{2,8},{3,9},... | collective-permute-start | bytes 393224 | tf_op jit(solution)/shard_map/ppermute | solution.py:353
  388.7 8.6 %shard_map.131 = bf16[1024,2048]{1,0:T(8,128)(2,1)} custom-call(s32[8,16]{1,0:T(8,128)S(1)} %copy-done.77, bf16[4,2,256,512]{3,2,1,0:T(8,128)(2,1)S(1)} %shard_map.119.x_ref, bf16[2,128,1024]{2,1,0:T(8,128)(2,1)S(1)} %copy-done.17, bf16[2,128,1024]{2,1,0:T(8,128)(2,1)S(1)} %copy-done.48, bf16[2,128,1024]{2,1,0:T(8,128)(2,1)S(1)} %copy-done.46, ...), custom_call_target="tpu_custom_call" | custom-call | flops 4294967296 | bytes 10485760 | tf_op jit(solution)/shard_map/pallas_call | solution.py:69
  (319 shorter events, 137.1 us)
Async XLA Ops:
  15.3 24.6 %collective-permute-start.2 = (bf16[256,512]{1,0:T(8,128)(2,1)S(1)}, bf16[256,512]{1,0:T(8,128)(2,1)S(1)}, u32[]{:S(2)}, u32[]{:S(2)}) collective-permute-start(bf16[256,512]{1,0:T(8,128)(2,1)S(1)} %collective-permute-done.rest_0_), channel_id=1, source_target_pairs={{0,4},{1,5},{2,6},{3,7},{4,0},{5,1},{6,2},{7,3},{8,12},{9,13},{10,... | collective-permute-start | bytes 786440 | tf_op jit(solution)/shard_map/ppermute | solution.py:325
  51.7 24.6 %collective-permute-start.10 = (bf16[256,1024]{1,0:T(8,128)(2,1)S(1)}, bf16[256,1024]{1,0:T(8,128)(2,1)S(1)}, u32[]{:S(2)}, u32[]{:S(2)}) collective-permute-start(bf16[256,1024]{1,0:T(8,128)(2,1)S(1)} %get-tuple-element.75), channel_id=1, source_target_pairs={{0,16},{8,24},{16,0},{24,8},{1,17},{9,25},{17,1},{25,9},{2,18},{10... | collective-permute-start | bytes 1572872 | tf_op jit(solution)/shard_map/ppermute | solution.py:336
  71.0 24.9 %collective-permute-start.15 = (bf16[256,1024]{1,0:T(8,128)(2,1)S(1)}, bf16[256,1024]{1,0:T(8,128)(2,1)S(1)}, u32[]{:S(2)}, u32[]{:S(2)}) collective-permute-start(bf16[256,1024]{1,0:T(8,128)(2,1)S(1)} %get-tuple-element.88), channel_id=1, source_target_pairs={{0,16},{8,24},{16,0},{24,8},{1,17},{9,25},{17,1},{25,9},{2,18},{10... | collective-permute-start | bytes 1572872 | tf_op jit(solution)/shard_map/ppermute | solution.py:336
  76.2 29.4 %collective-permute-start.8 = (bf16[256,1024]{1,0:T(8,128)(2,1)S(1)}, bf16[256,1024]{1,0:T(8,128)(2,1)S(1)}, u32[]{:S(2)}, u32[]{:S(2)}) collective-permute-start(bf16[256,1024]{1,0:T(8,128)(2,1)S(1)} %get-tuple-element.72), channel_id=1, source_target_pairs={{0,8},{8,0},{16,24},{24,16},{1,9},{9,1},{17,25},{25,17},{2,10},{10... | collective-permute-start | bytes 1572872 | tf_op jit(solution)/shard_map/ppermute | solution.py:336
  79.2 24.4 %collective-permute-start.19 = (bf16[256,512]{1,0:T(8,128)(2,1)S(1)}, bf16[256,512]{1,0:T(8,128)(2,1)}, u32[]{:S(2)}, u32[]{:S(2)}) collective-permute-start(bf16[256,512]{1,0:T(8,128)(2,1)S(1)} %collective-permute-done.18.rest_0_), channel_id=1, source_target_pairs={{0,2},{1,3},{2,0},{3,1},{4,6},{5,7},{6,4},{7,5},{8,10},{9,11},{10,... | collective-permute-start | bytes 786440 | tf_op jit(solution)/shard_map/ppermute | solution.py:325
  84.2 22.7 %collective-permute-start.12 = (bf16[256,1024]{1,0:T(8,128)(2,1)S(1)}, bf16[256,1024]{1,0:T(8,128)(2,1)S(1)}, u32[]{:S(2)}, u32[]{:S(2)}) collective-permute-start(bf16[256,1024]{1,0:T(8,128)(2,1)S(1)} %add_convert_fusion.7), channel_id=1, source_target_pairs={{0,8},{8,0},{16,24},{24,16},{1,9},{9,1},{17,25},{25,17},{2,10},{10... | collective-permute-start | bytes 1572872 | tf_op jit(solution)/shard_map/ppermute | solution.py:336
  96.7 23.3 %collective-permute-start.11 = (bf16[256,1024]{1,0:T(8,128)(2,1)}, bf16[256,1024]{1,0:T(8,128)(2,1)}, u32[]{:S(2)}, u32[]{:S(2)}) collective-permute-start(bf16[256,1024]{1,0:T(8,128)(2,1)} %add_convert_fusion.8), channel_id=1, source_target_pairs={{0,16},{8,24},{16,0},{24,8},{1,17},{9,25},{17,1},{25,9},{2,18},{10... | collective-permute-start | bytes 1572872 | tf_op jit(solution)/shard_map/ppermute | solution.py:336
  112.4 23.6 %collective-permute-start.13 = (bf16[256,1024]{1,0:T(8,128)(2,1)}, bf16[256,1024]{1,0:T(8,128)(2,1)}, u32[]{:S(2)}, u32[]{:S(2)}) collective-permute-start(bf16[256,1024]{1,0:T(8,128)(2,1)} %get-tuple-element.83), channel_id=1, source_target_pairs={{0,8},{8,0},{16,24},{24,16},{1,9},{9,1},{17,25},{25,17},{2,10},{10... | collective-permute-start | bytes 1572872 | tf_op jit(solution)/shard_map/ppermute | solution.py:336
  120.0 21.9 %collective-permute-start.26 = (bf16[256,1024]{1,0:T(8,128)(2,1)}, bf16[256,1024]{1,0:T(8,128)(2,1)S(1)}, u32[]{:S(2)}, u32[]{:S(2)}) collective-permute-start(bf16[256,1024]{1,0:T(8,128)(2,1)} %copy-done.75), channel_id=1, source_target_pairs={{0,16},{8,24},{16,0},{24,8},{1,17},{9,25},{17,1},{25,9},{2,18},{10... | collective-permute-start | bytes 1572872 | tf_op jit(solution)/shard_map/ppermute | solution.py:336
  125.3 21.8 %collective-permute-start.33 = (bf16[256,1024]{1,0:T(8,128)(2,1)S(1)}, bf16[256,1024]{1,0:T(8,128)(2,1)S(1)}, u32[]{:S(2)}, u32[]{:S(2)}) collective-permute-start(bf16[256,1024]{1,0:T(8,128)(2,1)S(1)} %add_convert_fusion.4), channel_id=1, source_target_pairs={{0,8},{8,0},{16,24},{24,16},{1,9},{9,1},{17,25},{25,17},{2,10},{10... | collective-permute-start | bytes 1572872 | tf_op jit(solution)/shard_map/ppermute | solution.py:336
  136.0 22.4 %collective-permute-start.28 = (bf16[256,1024]{1,0:T(8,128)(2,1)S(1)}, bf16[256,1024]{1,0:T(8,128)(2,1)S(1)}, u32[]{:S(2)}, u32[]{:S(2)}) collective-permute-start(bf16[256,1024]{1,0:T(8,128)(2,1)S(1)} %get-tuple-element.98), channel_id=1, source_target_pairs={{0,8},{8,0},{16,24},{24,16},{1,9},{9,1},{17,25},{25,17},{2,10},{10... | collective-permute-start | bytes 1572872 | tf_op jit(solution)/shard_map/ppermute | solution.py:336
  143.4 24.6 %collective-permute-start.17 = (bf16[256,1024]{1,0:T(8,128)(2,1)S(1)}, bf16[256,1024]{1,0:T(8,128)(2,1)S(1)}, u32[]{:S(2)}, u32[]{:S(2)}) collective-permute-start(bf16[256,1024]{1,0:T(8,128)(2,1)S(1)} %add_convert_fusion.6), channel_id=1, source_target_pairs={{0,16},{8,24},{16,0},{24,8},{1,17},{9,25},{17,1},{25,9},{2,18},{10... | collective-permute-start | bytes 1572872 | tf_op jit(solution)/shard_map/ppermute | solution.py:336
  147.2 22.5 %collective-permute-start.34 = (bf16[256,1024]{1,0:T(8,128)(2,1)S(1)}, bf16[256,1024]{1,0:T(8,128)(2,1)S(1)}, u32[]{:S(2)}, u32[]{:S(2)}) collective-permute-start(bf16[256,1024]{1,0:T(8,128)(2,1)S(1)} %get-tuple-element.108), channel_id=1, source_target_pairs={{0,8},{8,0},{16,24},{24,16},{1,9},{9,1},{17,25},{25,17},{2,10},{10... | collective-permute-start | bytes 1572872 | tf_op jit(solution)/shard_map/ppermute | solution.py:336
  189.8 22.8 %collective-permute-start.35 = (bf16[256,1024]{1,0:T(8,128)(2,1)S(1)}, bf16[256,1024]{1,0:T(8,128)(2,1)S(1)}, u32[]{:S(2)}, u32[]{:S(2)}) collective-permute-start(bf16[256,1024]{1,0:T(8,128)(2,1)S(1)} %get-tuple-element.113.rest_5_.rest_4_), channel_id=1, source_target_pairs={{0,8},{8,0},{16,24},{24,16},{1,9},{9,1},{17,25},{25,17},{2,10},{10... | collective-permute-start | bytes 1572872 | tf_op jit(solution)/shard_map/ppermute | solution.py:336
  191.3 25.1 %collective-permute-start.38 = (bf16[256,1024]{1,0:T(8,128)(2,1)S(1)}, bf16[256,1024]{1,0:T(8,128)(2,1)S(1)}, u32[]{:S(2)}, u32[]{:S(2)}) collective-permute-start(bf16[256,1024]{1,0:T(8,128)(2,1)S(1)} %get-tuple-element.113.rest_5_.rest_4_), channel_id=1, source_target_pairs={{0,16},{8,24},{16,0},{24,8},{1,17},{9,25},{17,1},{25,9},{2,18},{10... | collective-permute-start | bytes 1572872 | tf_op jit(solution)/shard_map/ppermute | solution.py:336
  214.9 23.7 %collective-permute-start.47 = (bf16[2,128,1024]{2,1,0:T(8,128)(2,1)S(1)}, bf16[2,128,1024]{2,1,0:T(8,128)(2,1)S(1)}, u32[]{:S(2)}, u32[]{:S(2)}) collective-permute-start(bf16[2,128,1024]{2,1,0:T(8,128)(2,1)S(1)} %pad_maximum_fusion.1.rest_6_.rest_4_), channel_id=1, source_target_pairs={{0,8},{8,0},{16,24},{24,16},{1,9},{9,1},{17,25},{25,17},{2,10},{10... | collective-permute-start | bytes 1572872 | tf_op jit(solution)/shard_map/ppermute | solution.py:336
  216.4 22.7 %collective-permute-start.46 = (bf16[2,128,1024]{2,1,0:T(8,128)(2,1)S(1)}, bf16[2,128,1024]{2,1,0:T(8,128)(2,1)S(1)}, u32[]{:S(2)}, u32[]{:S(2)}) collective-permute-start(bf16[2,128,1024]{2,1,0:T(8,128)(2,1)S(1)} %pad_maximum_fusion.rest_2_.rest_0_), channel_id=1, source_target_pairs={{0,16},{8,24},{16,0},{24,8},{1,17},{9,25},{17,1},{25,9},{2,18},{10... | collective-permute-start | bytes 1572872 | tf_op jit(solution)/shard_map/ppermute | solution.py:336
  227.4 24.6 %collective-permute-start.45 = (bf16[2,128,1024]{2,1,0:T(8,128)(2,1)S(1)}, bf16[2,128,1024]{2,1,0:T(8,128)(2,1)S(1)}, u32[]{:S(2)}, u32[]{:S(2)}) collective-permute-start(bf16[2,128,1024]{2,1,0:T(8,128)(2,1)S(1)} %pad_maximum_fusion.rest_2_.rest_0_), channel_id=1, source_target_pairs={{0,8},{8,0},{16,24},{24,16},{1,9},{9,1},{17,25},{25,17},{2,10},{10... | collective-permute-start | bytes 1572872 | tf_op jit(solution)/shard_map/ppermute | solution.py:336
  227.9 24.6 %collective-permute-start.49 = (bf16[2,128,1024]{2,1,0:T(8,128)(2,1)S(1)}, bf16[2,128,1024]{2,1,0:T(8,128)(2,1)S(1)}, u32[]{:S(2)}, u32[]{:S(2)}) collective-permute-start(bf16[2,128,1024]{2,1,0:T(8,128)(2,1)S(1)} %pad_maximum_fusion.1.rest_6_.rest_4_), channel_id=1, source_target_pairs={{0,16},{8,24},{16,0},{24,8},{1,17},{9,25},{17,1},{25,9},{2,18},{10... | collective-permute-start | bytes 1572872 | tf_op jit(solution)/shard_map/ppermute | solution.py:336
  251.9 41.7 %collective-permute-start.40 = (bf16[4,256,512]{2,1,0:T(8,128)(2,1)}, bf16[4,256,512]{2,1,0:T(8,128)(2,1)}, u32[]{:S(2)}, u32[]{:S(2)}) collective-permute-start(bf16[4,256,512]{2,1,0:T(8,128)(2,1)} %get-tuple-element.116), channel_id=1, source_target_pairs={{0,1},{1,0},{2,3},{3,2},{4,5},{5,4},{6,7},{7,6},{8,9},{9,8},{10,11... | collective-permute-start | bytes 3145736 | tf_op jit(solution)/shard_map/ppermute | solution.py:325
  252.0 37.2 %collective-permute-start.58 = (bf16[2,128,1024]{2,1,0:T(8,128)(2,1)}, bf16[2,128,1024]{2,1,0:T(8,128)(2,1)}, u32[]{:S(2)}, u32[]{:S(2)}) collective-permute-start(bf16[2,128,1024]{2,1,0:T(8,128)(2,1)} %pad_maximum_fusion.3.rest_6_.rest_12_), channel_id=1, source_target_pairs={{0,8},{8,0},{16,24},{24,16},{1,9},{9,1},{17,25},{25,17},{2,10},{10... | collective-permute-start | bytes 1572872 | tf_op jit(solution)/shard_map/ppermute | solution.py:336
  252.5 39.4 %collective-permute-start.57 = (bf16[2,128,1024]{2,1,0:T(8,128)(2,1)}, bf16[2,128,1024]{2,1,0:T(8,128)(2,1)}, u32[]{:S(2)}, u32[]{:S(2)}) collective-permute-start(bf16[2,128,1024]{2,1,0:T(8,128)(2,1)} %pad_maximum_fusion.2.rest_2_.rest_8_), channel_id=1, source_target_pairs={{0,16},{8,24},{16,0},{24,8},{1,17},{9,25},{17,1},{25,9},{2,18},{10... | collective-permute-start | bytes 1572872 | tf_op jit(solution)/shard_map/ppermute | solution.py:336
  269.4 22.8 %collective-permute-start.51 = (bf16[4,128,512]{2,1,0:T(8,128)(2,1)}, bf16[4,128,512]{2,1,0:T(8,128)(2,1)}, u32[]{:S(2)}, u32[]{:S(2)}) collective-permute-start(bf16[4,128,512]{2,1,0:T(8,128)(2,1)} %get-tuple-element.126), channel_id=1, source_target_pairs={{0,1},{1,0},{2,3},{3,2},{4,5},{5,4},{6,7},{7,6},{8,9},{9,8},{10,11... | collective-permute-start | bytes 1572872 | tf_op jit(solution)/shard_map/ppermute | solution.py:325
  291.9 21.5 %collective-permute-start.59 = (bf16[2,128,1024]{2,1,0:T(8,128)(2,1)}, bf16[2,128,1024]{2,1,0:T(8,128)(2,1)S(1)}, u32[]{:S(2)}, u32[]{:S(2)}) collective-permute-start(bf16[2,128,1024]{2,1,0:T(8,128)(2,1)} %collective-permute-done.57.rest_4_.rest_10_), channel_id=1, source_target_pairs={{0,8},{8,0},{16,24},{24,16},{1,9},{9,1},{17,25},{25,17},{2,10},{10... | collective-permute-start | bytes 1572872 | tf_op jit(solution)/shard_map/ppermute | solution.py:336
  292.2 23.4 %collective-permute-start.61 = (bf16[2,128,1024]{2,1,0:T(8,128)(2,1)}, bf16[2,128,1024]{2,1,0:T(8,128)(2,1)S(1)}, u32[]{:S(2)}, u32[]{:S(2)}) collective-permute-start(bf16[2,128,1024]{2,1,0:T(8,128)(2,1)} %collective-permute-done.58.rest_7_.rest_13_), channel_id=1, source_target_pairs={{0,16},{8,24},{16,0},{24,8},{1,17},{9,25},{17,1},{25,9},{2,18},{10... | collective-permute-start | bytes 1572872 | tf_op jit(solution)/shard_map/ppermute | solution.py:336
  294.3 31.9 %collective-permute-start.52 = (bf16[128,512]{1,0:T(8,128)(2,1)S(1)}, bf16[128,512]{1,0:T(8,128)(2,1)}, u32[]{:S(2)}, u32[]{:S(2)}) collective-permute-start(bf16[128,512]{1,0:T(8,128)(2,1)S(1)} %get-tuple-element.146), channel_id=1, source_target_pairs={{0,2},{1,3},{2,0},{3,1},{4,6},{5,7},{6,4},{7,5},{8,10},{9,11},{10,... | collective-permute-start | bytes 393224 | tf_op jit(solution)/shard_map/ppermute | solution.py:325
  302.6 24.6 %collective-permute-start.54 = (bf16[128,512]{1,0:T(8,128)(2,1)S(1)}, bf16[128,512]{1,0:T(8,128)(2,1)}, u32[]{:S(2)}, u32[]{:S(2)}) collective-permute-start(bf16[128,512]{1,0:T(8,128)(2,1)S(1)} %get-tuple-element.147), channel_id=1, source_target_pairs={{0,6},{1,7},{2,4},{3,5},{4,2},{5,3},{6,0},{7,1},{8,14},{9,15},{10,... | collective-permute-start | bytes 393224 | tf_op jit(solution)/shard_map/ppermute | solution.py:325
  304.9 24.9 %collective-permute-start.53 = (bf16[128,512]{1,0:T(8,128)(2,1)S(1)}, bf16[128,512]{1,0:T(8,128)(2,1)}, u32[]{:S(2)}, u32[]{:S(2)}) collective-permute-start(bf16[128,512]{1,0:T(8,128)(2,1)S(1)} %get-tuple-element.148), channel_id=1, source_target_pairs={{0,4},{1,5},{2,6},{3,7},{4,0},{5,1},{6,2},{7,3},{8,12},{9,13},{10,... | collective-permute-start | bytes 393224 | tf_op jit(solution)/shard_map/ppermute | solution.py:325
  325.2 35.7 %collective-permute-start.62 = (bf16[4,128,512]{2,1,0:T(8,128)(2,1)}, bf16[4,128,512]{2,1,0:T(8,128)(2,1)}, u32[]{:S(2)}, u32[]{:S(2)}) collective-permute-start(bf16[4,128,512]{2,1,0:T(8,128)(2,1)} %get-tuple-element.135), channel_id=1, source_target_pairs={{0,1},{1,0},{2,3},{3,2},{4,5},{5,4},{6,7},{7,6},{8,9},{9,8},{10,11... | collective-permute-start | bytes 1572872 | tf_op jit(solution)/shard_map/ppermute | solution.py:325
  327.2 26.0 %collective-permute-start.42 = (bf16[256,512]{1,0:T(8,128)(2,1)}, bf16[256,512]{1,0:T(8,128)(2,1)}, u32[]{:S(2)}, u32[]{:S(2)}) collective-permute-start(bf16[256,512]{1,0:T(8,128)(2,1)} %get-tuple-element.145), channel_id=1, source_target_pairs={{0,4},{1,5},{2,6},{3,7},{4,0},{5,1},{6,2},{7,3},{8,12},{9,13},{10,... | collective-permute-start | bytes 786440 | tf_op jit(solution)/shard_map/ppermute | solution.py:325
  331.1 66.2 %collective-permute-start.55 = (bf16[128,512]{1,0:T(8,128)(2,1)S(1)}, bf16[128,512]{1,0:T(8,128)(2,1)S(1)}, u32[]{:S(2)}, u32[]{:S(2)}) collective-permute-start(bf16[128,512]{1,0:T(8,128)(2,1)S(1)} %fusion.10), channel_id=1, source_target_pairs={{0,0},{1,1},{10,2},{11,3},{20,4},{21,5},{30,6},{31,7},{2,8},{3,9},... | collective-permute-start | bytes 393224 | tf_op jit(solution)/shard_map/ppermute | solution.py:353
  354.5 42.8 %collective-permute-start.44 = (bf16[256,512]{1,0:T(8,128)(2,1)S(1)}, bf16[256,512]{1,0:T(8,128)(2,1)S(1)}, u32[]{:S(2)}, u32[]{:S(2)}) collective-permute-start(bf16[256,512]{1,0:T(8,128)(2,1)S(1)} %fusion.4), channel_id=1, source_target_pairs={{0,0},{1,1},{10,2},{11,3},{20,4},{21,5},{30,6},{31,7},{2,8},{3,9},... | collective-permute-start | bytes 786440 | tf_op jit(solution)/shard_map/ppermute | solution.py:353
  (123 other events, 1994.0 us)
